TPU v7x, 32 devices: a whole 2x2x4 slice. The times are simulated.
32 devices in a mesh: seq: 8 (over y, x, core), red: 4 (over z).
Axes of the slice: x: 2, y: 2, z: 4, core: 2. Of those that a mesh axis runs over, the one named last changes fastest.
Arguments:
- token_ids: int32 [1024], P('seq'), may hold values from 0 to 511
- embedding: bfloat16 [512, 4096], P(None, 'red'), may hold values from -6 to 6
- proj_weight: bfloat16 [4096, 3, 4, 256], P('red', None, None, 'seq'), may hold values from -0.09375 to 0.09375
- filters: float32 [1024, 1024], P('seq', 'red'), may hold values from -1 to 1
- cotangent: float32 [1024, 1024], P('seq', 'red'), may hold values from -6 to 6
Outputs:
- output: float32 [1024, 1024], P('seq', 'red')
- filter_grad: float32 [1024, 1024], P('seq', 'red')
- branch_grads: bfloat16 [1024, 3, 1024], P('seq', None, 'red')
- weight_grad: float32 [4096, 3, 4, 256], P('red', None, None, 'seq')
All inputs are finite; a program needn't handle non-finite values.
Results may differ from a plain program's by a relative error of at most 0.0029.
Values sent between devices are 32-bit elements; how exact they have to be, the bound alone decides.
A program may use at most 64 MiB of HBM per device.

v0:
```python
import functools
import math

import jax
import jax.numpy as jnp
import numpy as np
from jax import lax
from jax.experimental import pallas as pl
from jax.experimental.pallas import tpu as pltpu
from jax.sharding import PartitionSpec as P

precise_mode = lax.Precision.HIGHEST
MESH = pl.DeviceIdType.MESH
VMEM = pl.BlockSpec(memory_space=pltpu.VMEM)
CHUNKS = 1
NN = (((1,), (0,)), ((), ()))
NT = (((1,), (1,)), ((), ()))


def split(value):
    high = value.astype(jnp.bfloat16)
    low = (value - high.astype(jnp.float32)).astype(jnp.bfloat16)
    return high, low


def dot(left, right, dims=NN):
    return lax.dot_general(left, right, dims, preferred_element_type=jnp.float32)


def dot_split(value, matrix, dims=NN):
    high, low = split(value)
    both = dot(jnp.concatenate([high, low], axis=0), matrix, dims)
    rows = value.shape[0]
    return both[:rows] + both[rows:]


def dot_both(value, matrix_high, matrix_low, dims=NN):
    high, _ = split(value)
    return dot_split(value, matrix_high, dims) + dot(high, matrix_low, dims)


def transform_tables(block, blocks):
    total = 2 * blocks * block
    place = np.arange(block)
    half = block // 2
    tables = np.zeros((blocks, 2 * block, 2 * block))
    even = 2 * np.pi * ((2 * blocks * place[:, None] * np.arange(half)[None, :]) % total) / total
    odd = 2 * np.pi * ((place[:, None] * (blocks + 2 * blocks * np.arange(half))[None, :]) % total) / total
    tables[0, :block, :half] = np.cos(even)
    tables[0, :block, block : block + half] = np.sin(even)
    tables[0, :block, block] = 1.0 - 2.0 * (place % 2)
    tables[0, block:, half:block] = np.cos(odd)
    tables[0, block:, block + half :] = np.sin(odd)
    for residue in range(1, blocks):
        freq = residue + 2 * blocks * np.arange(block)
        psi = 2 * np.pi * ((place[:, None] * freq[None, :]) % total) / total
        tables[residue, :block, :block] = np.cos(psi)
        tables[residue, :block, block:] = np.sin(psi)
        tables[residue, block:, :block] = -np.sin(psi)
        tables[residue, block:, block:] = np.cos(psi)
    tables = tables.astype(np.float32)
    high = tables.astype(jnp.bfloat16)
    low = (tables - high.astype(np.float32)).astype(jnp.bfloat16)
    return high, low


def phases(residue, blocks):
    if residue == 0:
        return [1.0] * blocks, [(-1.0) ** index for index in range(blocks)]
    turn = [math.pi * ((residue * index) % (2 * blocks)) / blocks for index in range(blocks)]
    return [math.cos(a) for a in turn], [math.sin(a) for a in turn]


def weighted(terms, weights):
    total = None
    for term, weight in zip(terms, weights):
        if abs(weight) < 1e-12:
            continue
        part = term if weight == 1.0 else term * weight
        total = part if total is None else total + part
    return total


def convolve(signals, high_ref, low_ref, piece, beside):
    blocks, double, _ = high_ref.shape
    block = double // 2
    pieces = [signals[:, index * block : (index + 1) * block] for index in range(blocks)]
    results = [None] * blocks
    scale = 1.0 / (blocks * block)
    for residue in range(blocks):
        if residue == blocks // 2:
            beside()
        cosines, sines = phases(residue, blocks)
        packed = jnp.concatenate([weighted(pieces, cosines), weighted(pieces, sines)], axis=1)
        spectrum = dot_both(packed, high_ref[residue], low_ref[residue])
        cos_part = spectrum[:, :block]
        sin_part = spectrum[:, block:]
        fc, ic, uc = (cos_part[at * piece : (at + 1) * piece] for at in range(3))
        fs, i_s, us = (sin_part[at * piece : (at + 1) * piece] for at in range(3))
        cc = [fc * ic, fc * uc, uc * ic]
        ss = [fs * i_s, fs * us, us * i_s]
        signs = [-1.0, 1.0, 1.0]
        new_cos = [c + sign * s for c, s, sign in zip(cc, ss, signs)]
        new_sin = [fc * i_s + fs * ic, fc * us - fs * uc, us * ic - uc * i_s]
        new_cos = jnp.concatenate(new_cos, axis=0)
        new_sin = jnp.concatenate(new_sin, axis=0)
        if residue == 0:
            first = lax.broadcasted_iota(jnp.int32, new_cos.shape, 1) == 0
            new_cos = jnp.where(first, 0.5 * jnp.concatenate(cc, axis=0), new_cos)
            new_sin = jnp.where(first, 0.5 * jnp.concatenate(ss, axis=0), new_sin)
        joined = jnp.concatenate([new_cos, new_sin], axis=1) * scale
        back = dot_both(joined, high_ref[residue], low_ref[residue], NT)
        first_half = back[:, :block]
        second_half = back[:, block:]
        for index in range(blocks):
            term = weighted([first_half, second_half], [cosines[index], sines[index]])
            results[index] = term if results[index] is None else results[index] + term
    return results


def greet(devices, count):
    me = lax.axis_index("seq")
    spot = lax.axis_index("red")
    barrier = pltpu.get_barrier_semaphore()
    for step in range(1, devices):
        peer = lax.rem(me + step, devices)
        pl.semaphore_signal(barrier, inc=1, device_id={"seq": peer}, device_id_type=MESH)

    @pl.when(spot > 0)
    def _():
        pl.semaphore_signal(barrier, inc=1, device_id={"red": spot - 1}, device_id_type=MESH)

    @pl.when(spot < count - 1)
    def _():
        pl.semaphore_signal(barrier, inc=1, device_id={"red": spot + 1}, device_id_type=MESH)


def meet(devices, count):
    spot = lax.axis_index("red")
    neighbours = jnp.where(spot > 0, 1, 0) + jnp.where(spot < count - 1, 1, 0)
    pl.semaphore_wait(pltpu.get_barrier_semaphore(), devices - 1 + neighbours)


def exchange(devices, source, target, send_sem, recv_sem, base):
    me = lax.axis_index("seq")
    copies = []
    for step in range(1, devices):
        peer = lax.rem(me + step, devices)
        copy = pltpu.make_async_remote_copy(
            src_ref=source(peer),
            dst_ref=target(me),
            send_sem=send_sem.at[base + step - 1],
            recv_sem=recv_sem.at[base + step - 1],
            device_id={"seq": peer},
            device_id_type=MESH,
        )
        copy.start()
        copies.append(copy)
    return copies


def main_kernel(
    devices, count, chunks, scale_factor,
    tok_ref, emb_ref, wt_ref, filt_ref, cot_ref, high_hbm, low_hbm,
    recv_ref, all_ref,
    part, from_left, from_right, out_sig, sig, sending, one_hot, high_ref, low_ref,
    table_sem, sig_send, sig_recv, res_send, res_recv,
    right_send, right_recv, left_send, left_recv,
    up_send, up_recv, down_send, down_recv,
):
    me = lax.axis_index("seq")
    spot = lax.axis_index("red")
    branches, _, piece, _ = wt_ref.shape
    tok_count, width = filt_ref.shape
    vocabulary = emb_ref.shape[0]
    sub = piece // chunks
    greet(devices, count)
    tables = [
        pltpu.make_async_copy(high_hbm, high_ref, table_sem.at[0]),
        pltpu.make_async_copy(low_hbm, low_ref, table_sem.at[1]),
    ]
    for copy in tables:
        copy.start()
    above_spot = jnp.minimum(spot + 1, count - 1)
    below_spot = jnp.maximum(spot - 1, 0)

    def hop(source, target, slot, sends, recvs, neighbour):
        return pltpu.make_async_remote_copy(
            src_ref=source.at[slot],
            dst_ref=target.at[slot],
            send_sem=sends.at[slot],
            recv_sem=recvs.at[slot],
            device_id={"red": neighbour},
            device_id_type=MESH,
        )

    def place(chunk, branch):
        return (chunk * branches + branch) * count

    def right(slot):
        return hop(part, from_left, slot, right_send, right_recv, above_spot)

    def left(slot):
        return hop(part, from_right, slot, left_send, left_recv, below_spot)

    def up(slot):
        return hop(all_ref, all_ref, slot, up_send, up_recv, above_spot)

    def down(slot):
        return hop(all_ref, all_ref, slot, down_send, down_recv, below_spot)

    def products(chunk):
        table = emb_ref[...]
        for group in range(count):
            rows = [wt_ref[b, group, chunk * sub : (chunk + 1) * sub] for b in range(branches)]
            product = dot(jnp.concatenate(rows, axis=0), table, NT)
            for b in range(branches):
                part[place(chunk, b) + group] = product[b * sub : (b + 1) * sub]

    def first_hops(chunk):
        bases = [place(chunk, branch) for branch in range(branches)]

        @pl.when(spot == 0)
        def _():
            for goal in range(count - 1, 0, -1):
                for base in bases:
                    right(base + goal).start()

        @pl.when(spot == count - 1)
        def _():
            for goal in range(count - 1):
                for base in bases:
                    left(base + goal).start()

    def middle_hops(chunk):
        for tick in range(1, count - 1):
            for branch in range(branches):
                later_hop(place(chunk, branch), tick)

    def later_hop(base, tick):
        goal = count - 1 - (tick - spot)

        @pl.when((spot > 0) & (tick >= spot) & (spot < goal))
        def _():
            right(base + goal).wait_recv()
            part[base + goal] = part[base + goal] + from_left[base + goal]
            right(base + goal).start()

        other = tick - (count - 1 - spot)

        @pl.when((spot < count - 1) & (other >= 0) & (spot > other))
        def _():
            left(base + other).wait_recv()
            part[base + other] = part[base + other] + from_right[base + other]
            left(base + other).start()

    def arrive(chunk):
        for branch in range(branches):
            slot = place(chunk, branch) + spot

            @pl.when(spot > 0)
            def _():
                right(slot).wait_recv()
                part[slot] = part[slot] + from_left[slot]

            @pl.when(spot < count - 1)
            def _():
                left(slot).wait_recv()
                part[slot] = part[slot] + from_right[slot]

        slots = [place(chunk, branch) + spot for branch in range(branches)]
        return jnp.concatenate([part[slot] for slot in slots], axis=0)

    def share(chunk):
        for branch in range(branches):
            slot = place(chunk, branch) + spot

            @pl.when(spot < count - 1)
            def _():
                up(slot).start()

            @pl.when(spot > 0)
            def _():
                down(slot).start()

    def relay(chunk, step):
        for branch in range(branches):
            relay_block(place(chunk, branch), step)

    def relay_block(base, step):
        below = spot - step

        @pl.when(below >= 0)
        def _():
            up(base + below).wait_recv()

            @pl.when(spot < count - 1)
            def _():
                up(base + below).start()

        above = spot + step

        @pl.when(above < count)
        def _():
            down(base + above).wait_recv()

            @pl.when(spot > 0)
            def _():
                down(base + above).start()

    def signal_rows(start, rows):
        return jnp.concatenate([sig[at, start : start + rows] for at in range(devices)], axis=1)

    def channels(chunk, own, beside):
        projected = dot_split(own, one_hot[...])
        queries = projected[:sub]
        key_rows = projected[sub : 2 * sub]
        value_rows = projected[2 * sub :]
        filters = signal_rows(chunk * sub, sub)
        cotangent = signal_rows(piece + chunk * sub, sub)
        signals = jnp.concatenate([filters, key_rows * value_rows, cotangent * queries], axis=0)
        results = convolve(signals, high_ref, low_ref, sub, beside)
        rounded = []
        for at in range(devices):
            lanes = slice(at * tok_count, (at + 1) * tok_count)
            conv = results[at][:sub]
            grad_inner = results[at][sub : 2 * sub]
            grads = jnp.concatenate(
                [
                    cotangent[:, lanes] * conv,
                    grad_inner * value_rows[:, lanes],
                    grad_inner * key_rows[:, lanes],
                ],
                axis=0,
            ).astype(jnp.bfloat16)
            rounded.append(grads)
            sending[chunk, at, :sub] = queries[:, lanes] * conv
            sending[chunk, at, sub : 2 * sub] = results[at][2 * sub :] * scale_factor
            sending[chunk, at, 2 * sub :] = grads.astype(jnp.float32)
        sums = dot(jnp.concatenate(rounded, axis=1), one_hot[...], NT)
        for b in range(branches):
            all_ref[place(chunk, b) + spot] = sums[b * sub : (b + 1) * sub]

    filt_t = filt_ref[...].T
    cot_t = cot_ref[...].T
    tok_rows = jnp.broadcast_to(tok_ref[...].astype(jnp.float32), (8, tok_count))
    for peer in range(devices):
        out_sig[peer, :piece] = filt_t[peer * piece : (peer + 1) * piece]
        out_sig[peer, piece : 2 * piece] = cot_t[peer * piece : (peer + 1) * piece]
        out_sig[peer, 2 * piece :] = tok_rows
    products(0)
    meet(devices, count)
    first_hops(0)
    copies = exchange(devices, out_sig.at.__getitem__, sig.at.__getitem__, sig_send, sig_recv, 0)
    for chunk in range(1, chunks):
        products(chunk)
        first_hops(chunk)
    sig[me] = out_sig[me]
    for copy in copies:
        copy.wait_recv()
    ids = signal_rows(2 * piece, 1).astype(jnp.int32)
    vocab_rows = lax.broadcasted_iota(jnp.int32, (vocabulary, devices * tok_count), 0)
    one_hot[...] = jnp.where(vocab_rows == ids, 1.0, 0.0).astype(jnp.bfloat16)
    sent = list(copies)
    arrivals = []
    for chunk in range(chunks):
        middle_hops(chunk)
        if chunk > 0:
            relay(chunk - 1, 1)
        own = arrive(chunk)
        if chunk == 0:
            for copy in tables:
                copy.wait()

        def beside(chunk=chunk):
            if chunk > 0 and count > 2:
                relay(chunk - 1, 2)

        channels(chunk, own, beside)
        share(chunk)
        more = exchange(
            devices,
            lambda peer, chunk=chunk: sending.at[chunk, peer],
            lambda slot, chunk=chunk: recv_ref.at[chunk, slot],
            res_send, res_recv, chunk * (devices - 1),
        )
        recv_ref[chunk, me] = sending[chunk, me]
        sent += more
        arrivals += more
        if chunk > 0:
            for step in range(3, count):
                relay(chunk - 1, step)
    for step in range(1, count):
        relay(chunks - 1, step)
    for base in range(0, chunks * branches * count, count):
        for goal in range(count):
            @pl.when(spot < goal)
            def _():
                right(base + goal).wait_send()

            @pl.when(spot > goal)
            def _():
                left(base + goal).wait_send()

        for step in range(count):
            @pl.when((spot - step >= 0) & (spot < count - 1))
            def _():
                up(base + spot - step).wait_send()

            @pl.when((spot + step < count) & (spot > 0))
            def _():
                down(base + spot + step).wait_send()

    for copy in sent:
        copy.wait_send()
    for copy in arrivals:
        copy.wait_recv()


def final_kernel(scale_factor, emb_ref, recv_ref, all_ref, out_ref, filt_ref, grads_ref, weight_ref):
    chunks, devices, rows, _ = recv_ref.shape
    sub = rows // 5
    count = all_ref.shape[0] // (chunks * 3)
    table = emb_ref[...]
    for chunk in range(chunks):
        for group in range(count):
            blocks = [all_ref[(chunk * 3 + branch) * count + group] for branch in range(3)]
            product = dot_split(jnp.concatenate(blocks, axis=0), table) * scale_factor
            for branch in range(3):
                weight_ref[branch, group, chunk * sub : (chunk + 1) * sub] = product[
                    branch * sub : (branch + 1) * sub
                ]

    def positions(at):
        parts = [
            recv_ref[chunk, peer, at * sub : (at + 1) * sub]
            for peer in range(devices)
            for chunk in range(chunks)
        ]
        return jnp.concatenate(parts, axis=0).T

    out_ref[...] = positions(0)
    filt_ref[...] = positions(1)
    for branch in range(3):
        grads_ref[branch] = positions(2 + branch).astype(jnp.bfloat16)


def kernel_shards(devices, count, token_ids, embedding, proj_weight, filters, cotangent):
    tok_count, width = filters.shape
    vocabulary, depth = embedding.shape
    _, branches, _, piece = proj_weight.shape
    scale_factor = float(tok_count * devices) ** (-0.5)
    chunks = CHUNKS
    rows = piece // chunks
    f32 = jnp.float32
    dma = pltpu.SemaphoreType.DMA
    weight_t = jnp.transpose(proj_weight, (1, 2, 3, 0))
    high, low = transform_tables(tok_count, devices)
    block = (chunks * branches * count, rows, vocabulary)
    message = (devices, 2 * piece + 8, tok_count)
    answer = (chunks, devices, 5 * piece // chunks, tok_count)
    received, all_sums = pl.pallas_call(
        functools.partial(main_kernel, devices, count, chunks, scale_factor),
        out_shape=(jax.ShapeDtypeStruct(answer, f32), jax.ShapeDtypeStruct(block, f32)),
        in_specs=[VMEM] * 5 + [pl.BlockSpec(memory_space=pl.ANY)] * 2,
        out_specs=(VMEM, VMEM),
        scratch_shapes=[
            pltpu.VMEM(block, f32),
            pltpu.VMEM(block, f32),
            pltpu.VMEM(block, f32),
            pltpu.VMEM(message, f32),
            pltpu.VMEM(message, f32),
            pltpu.VMEM(answer, f32),
            pltpu.VMEM((vocabulary, devices * tok_count), jnp.bfloat16),
            pltpu.VMEM(high.shape, jnp.bfloat16),
            pltpu.VMEM(low.shape, jnp.bfloat16),
            dma((2,)),
            dma((devices - 1,)),
            dma((devices - 1,)),
            dma((chunks * (devices - 1),)),
            dma((chunks * (devices - 1),)),
        ]
        + [dma((chunks * branches * count,))] * 8,
        compiler_params=pltpu.CompilerParams(collective_id=0, has_side_effects=True),
        name="hyena_exchange",
    )(
        token_ids.reshape(1, tok_count), embedding, weight_t, filters, cotangent,
        jnp.asarray(high), jnp.asarray(low),
    )
    output, filter_grad, grads, weight = pl.pallas_call(
        functools.partial(final_kernel, scale_factor),
        out_shape=(
            jax.ShapeDtypeStruct((tok_count, width), f32),
            jax.ShapeDtypeStruct((tok_count, width), f32),
            jax.ShapeDtypeStruct((branches, tok_count, width), jnp.bfloat16),
            jax.ShapeDtypeStruct((branches, count, piece, depth), f32),
        ),
        in_specs=[VMEM] * 3,
        out_specs=(VMEM,) * 4,
        name="finish",
    )(embedding, received, all_sums)
    return (
        output,
        filter_grad,
        jnp.transpose(grads, (1, 0, 2)),
        jnp.transpose(weight, (3, 0, 1, 2)),
    )


def fits_kernels(devices, count, token_ids, embedding, proj_weight, filters):
    tok_count, width = filters.shape
    vocabulary, depth = embedding.shape
    _, branches, red_count, piece = proj_weight.shape
    lanes = (tok_count, vocabulary, depth)
    aligned = all(size % 128 == 0 for size in lanes) and piece % (16 * CHUNKS) == 0
    tables = devices * (2 * tok_count) ** 2 * 4
    one_hot = vocabulary * tok_count * devices * 8
    held = 4 * branches * piece * vocabulary * (3 * count + 2)
    return (
        aligned
        and branches == 3
        and red_count == count
        and width == devices * piece
        and tables + one_hot + held < 40 * 2**20
    )


def angles(numbers, modulus, direction):
    phase = (numbers % modulus).astype(jnp.float32) * (direction * 2.0 * math.pi / modulus)
    return (jnp.cos(phase), jnp.sin(phase))


def rotate(real_part, imag_part, cosine, sine_part):
    return (real_part * cosine - imag_part * sine_part, real_part * sine_part + imag_part * cosine)


def complex_einsum(formula, matrix, values):
    mat_real, mat_imag = matrix
    val_real, val_imag = values
    real_out = jnp.einsum(formula, mat_real, val_real, precision=precise_mode) - jnp.einsum(
        formula, mat_imag, val_imag, precision=precise_mode
    )
    imag_out = jnp.einsum(formula, mat_real, val_imag, precision=precise_mode) + jnp.einsum(
        formula, mat_imag, val_real, precision=precise_mode
    )
    return (real_out, imag_out)


def factors(length_total):
    first_factor = 1
    for candidate in range(1, math.isqrt(length_total) + 1):
        if length_total % candidate == 0:
            first_factor = candidate
    return (first_factor, length_total // first_factor)


def combine_spectra(spec_real, spec_imag, width):
    filt_re = spec_real[..., :width]
    inner_re = spec_real[..., width : 2 * width]
    up_re = spec_real[..., 2 * width :]
    filt_im = spec_imag[..., :width]
    inner_im = spec_imag[..., width : 2 * width]
    up_im = spec_imag[..., 2 * width :]
    joined_real = jnp.concatenate(
        [
            filt_re * inner_re - filt_im * inner_im,
            filt_re * up_re + filt_im * up_im,
            up_re * inner_re + up_im * inner_im,
        ],
        axis=-1,
    )
    joined_imag = jnp.concatenate(
        [
            filt_re * inner_im + filt_im * inner_re,
            filt_re * up_im - filt_im * up_re,
            up_im * inner_re - up_re * inner_im,
        ],
        axis=-1,
    )
    return (joined_real, joined_imag)


def local_convolve(signals):
    length, branch_count, narrow = signals.shape
    total = 2 * length
    first_factor, second_factor = factors(total)
    flat = signals.reshape(length, branch_count * narrow)
    padded = jnp.concatenate([flat, jnp.zeros_like(flat)], axis=0).reshape(
        first_factor, second_factor, branch_count * narrow
    )
    first_index = jnp.arange(first_factor, dtype=jnp.int32)
    second_index = jnp.arange(second_factor, dtype=jnp.int32)
    cosine, sine_part = angles(first_index[:, None] * first_index[None, :], first_factor, -1.0)
    real_part = jnp.einsum("kn,nbm->kbm", cosine, padded, precision=precise_mode)
    imag_part = jnp.einsum("kn,nbm->kbm", sine_part, padded, precision=precise_mode)
    cosine, sine_part = angles(first_index[:, None] * second_index[None, :], total, -1.0)
    real_part, imag_part = rotate(real_part, imag_part, cosine[:, :, None], sine_part[:, :, None])
    real_part, imag_part = complex_einsum(
        "lb,kbm->klm",
        angles(second_index[:, None] * second_index[None, :], second_factor, -1.0),
        (real_part, imag_part),
    )
    real_part, imag_part = combine_spectra(real_part, imag_part, narrow)
    real_part, imag_part = complex_einsum(
        "bl,klm->kbm",
        angles(second_index[:, None] * second_index[None, :], second_factor, 1.0),
        (real_part, imag_part),
    )
    cosine, sine_part = angles(first_index[:, None] * second_index[None, :], total, 1.0)
    real_part, imag_part = rotate(real_part, imag_part, cosine[:, :, None], sine_part[:, :, None])
    cosine, sine_part = angles(first_index[:, None] * first_index[None, :], first_factor, 1.0)
    result = jnp.einsum("nk,kbm->nbm", cosine, real_part, precision=precise_mode) - jnp.einsum(
        "nk,kbm->nbm", sine_part, imag_part, precision=precise_mode
    )
    result = result.reshape(total, branch_count * narrow)[:length] / total
    return result.reshape(length, branch_count, narrow)


def shards(token_ids, embedding, proj_weight, filters, cotangent):
    tok_count = token_ids.shape[0]
    devices = lax.axis_size("seq")
    count = lax.axis_size("red")
    if fits_kernels(devices, count, token_ids, embedding, proj_weight, filters):
        return kernel_shards(
            devices, count, token_ids, embedding, proj_weight, filters, cotangent
        )
    width = filters.shape[1]
    vocabulary = embedding.shape[0]
    width_rows, branches, red_count, piece = proj_weight.shape
    scale_factor = float(tok_count * devices) ** (-0.5)
    table = jnp.dot(
        embedding,
        proj_weight.reshape(width_rows, branches * red_count * piece),
        preferred_element_type=jnp.float32,
    )
    table = table.reshape(vocabulary, branches, red_count, piece)
    own_table = lax.psum_scatter(table, "red", scatter_dimension=2, tiled=True)
    full_table = lax.all_gather(own_table, "seq", axis=3, tiled=True)
    projected = jnp.take(full_table, token_ids, axis=0)
    projected = projected.reshape(tok_count, branches, width)
    queries = projected[:, 0]
    key_rows = projected[:, 1]
    value_rows = projected[:, 2]
    inner = key_rows * value_rows
    upstream = cotangent * queries
    stacked = jnp.stack([filters, inner, upstream], axis=1)
    whole_length = lax.all_to_all(stacked, "seq", split_axis=2, concat_axis=0, tiled=True)
    results = local_convolve(whole_length)
    returned = lax.all_to_all(results, "seq", split_axis=0, concat_axis=2, tiled=True)
    conv = returned[:, 0]
    grad_inner = returned[:, 1]
    filter_raw = returned[:, 2]
    output = queries * conv
    filter_grad = filter_raw * scale_factor
    branch_grads = jnp.stack(
        [cotangent * conv, grad_inner * value_rows, grad_inner * key_rows], axis=1
    ).astype(jnp.bfloat16)
    one_hot = (token_ids[:, None] == lax.iota(jnp.int32, vocabulary)[None, :]).astype(jnp.bfloat16)
    token_sums = lax.dot_general(
        one_hot,
        branch_grads.reshape(tok_count, branches * width),
        (((0,), (0,)), ((), ())),
        preferred_element_type=jnp.float32,
    )
    summed = lax.psum_scatter(
        token_sums.reshape(vocabulary, branches, width), "seq", scatter_dimension=2, tiled=True
    )
    gathered = lax.all_gather(summed[:, :, None, :], "red", axis=2, tiled=True)
    weight_grad = (
        lax.dot_general(
            embedding.astype(jnp.float32),
            gathered.reshape(vocabulary, branches * red_count * piece),
            (((0,), (0,)), ((), ())),
            precision=precise_mode,
        )
        * scale_factor
    )
    return (
        output,
        filter_grad,
        branch_grads,
        weight_grad.reshape(width_rows, branches, red_count, piece),
    )


def solution(mesh):
    in_specs = (
        P("seq"),
        P(None, "red"),
        P("red", None, None, "seq"),
        P("seq", "red"),
        P("seq", "red"),
    )
    out_specs = (
        P("seq", "red"),
        P("seq", "red"),
        P("seq", None, "red"),
        P("red", None, None, "seq"),
    )
    return jax.shard_map(shards, mesh=mesh, in_specs=in_specs, out_specs=out_specs, check_vma=False)
```

profile of v0, /device:TPU:0, one launch (start us, length us, event | category | flops | bytes accessed | tf_op | source)
XLA Modules:
  0.0 45.3 jit_solution(120432655009519807)
XLA Ops:
  0.6 40.9 %hyena_exchange.1 = (f32[1,8,160,128]{3,2,1,0:T(8,128)}, f32[12,32,512]{2,1,0:T(8,128)}) custom-call(s32[1,128]{1,0:T(1,128)} %bitcast.5, bf16[512,1024]{1,0:T(8,128)(2,1)} %emb_ref.3, bf16[3,4,32,1024]{3,2,1,0:T(8,128)(2,1)} %bitcast.4, f32[128,256]{1,0:T(8,128)} %filt_ref.1, f32[128,256]{1,0:T(8,128)} %cot_ref.1, ...), custom_call_target="tpu_custom_call" | custom-call | tf_op jit(solution)/shard_map/hyena_exchange/pallas_call | solution.py:462
  41.5 3.8 %finish.1 = (f32[128,256]{1,0:T(8,128)}, f32[128,256]{1,0:T(8,128)}, bf16[3,128,256]{2,1,0:T(8,128)(2,1)}, f32[3,4,32,1024]{3,2,1,0:T(8,128)}) custom-call(bf16[512,1024]{1,0:T(8,128)(2,1)} %emb_ref.3, f32[1,8,160,128]{3,2,1,0:T(8,128)} %get-tuple-element.10.recv_ref, f32[12,32,512]{2,1,0:T(8,128)} %get-tuple-element.11.all_ref), custom_call_target="tpu_custom_call" | custom-call | tf_op jit(solution)/shard_map/finish/pallas_call | solution.py:490
where the time goes:
time: 45.5 us; the launch traced here: 45.3 us
  Pallas kernels  44.7 us (98%)
  between operations  0.64 us (1%)
    pallas_call x1, Pallas kernels, kernel_shards(): pl.pallas_call(functools.partial(main_kernel, devices, count, chunks, sca...  40.9 us
    pallas_call x1, Pallas kernels, kernel_shards(): pl.pallas_call(functools.partial(final_kernel, scale_factor), out_shape=(...  3.83 us

commit v1 on v0

v1 whole, which is shorter than its diff:
```python
import functools
import math

import jax
import jax.numpy as jnp
import numpy as np
from jax import lax
from jax.experimental import pallas as pl
from jax.experimental.pallas import tpu as pltpu
from jax.sharding import PartitionSpec as P

precise_mode = lax.Precision.HIGHEST
MESH = pl.DeviceIdType.MESH
VMEM = pl.BlockSpec(memory_space=pltpu.VMEM)
SHARES = (1,)
VMEM_BYTES = 67043328
NN = (((1,), (0,)), ((), ()))
NT = (((1,), (1,)), ((), ()))


def dot(left, right, dims=NN):
    return lax.dot_general(left, right, dims, preferred_element_type=jnp.float32)


def stack_split(value):
    high = value.astype(jnp.bfloat16).astype(jnp.float32)
    return jnp.concatenate([high, value - high], axis=0).astype(jnp.bfloat16)


def dot_split(value, matrix, dims=NN):
    both = dot(stack_split(value), matrix, dims)
    rows = value.shape[0]
    return both[:rows] + both[rows:]


def dot_both(value, matrix_high, matrix_low, dims=NN):
    high = value.astype(jnp.bfloat16)
    return dot_split(value, matrix_high, dims) + dot(high, matrix_low, dims)


def transform_tables(block, blocks):
    total = 2 * blocks * block
    place = np.arange(block)
    half = block // 2
    tables = np.zeros((2, 2 * block, 2 * block))
    even = 2 * np.pi * ((2 * blocks * place[:, None] * np.arange(half)[None, :]) % total) / total
    odd = 2 * np.pi * ((place[:, None] * (blocks + 2 * blocks * np.arange(half))[None, :]) % total) / total
    tables[0, :block, :half] = np.cos(even)
    tables[0, :block, block : block + half] = np.sin(even)
    tables[0, :block, block] = 1.0 - 2.0 * (place % 2)
    tables[0, block:, half:block] = np.cos(odd)
    tables[0, block:, block + half :] = np.sin(odd)
    psi = 2 * np.pi * ((place[:, None] * place[None, :]) % block) / block
    tables[1, :block, :block] = np.cos(psi)
    tables[1, :block, block:] = np.sin(psi)
    tables[1, block:, :block] = -np.sin(psi)
    tables[1, block:, block:] = np.cos(psi)
    tables = tables.astype(np.float32)
    high = tables.astype(jnp.bfloat16)
    low = (tables - high.astype(np.float32)).astype(jnp.bfloat16)
    alpha = 2 * np.pi * np.arange(blocks)[:, None] * place[None, :] / total
    return high, low, np.concatenate([np.cos(alpha), np.sin(alpha)]).astype(np.float32)


def phases(residue, blocks):
    if residue == 0:
        return [1.0] * blocks, [(-1.0) ** index for index in range(blocks)]
    turn = [math.pi * ((residue * index) % (2 * blocks)) / blocks for index in range(blocks)]
    return [math.cos(a) for a in turn], [math.sin(a) for a in turn]


def weighted(terms, weights):
    total = None
    for term, weight in zip(terms, weights):
        if abs(weight) < 1e-12:
            continue
        part = term if weight == 1.0 else (-term if weight == -1.0 else term * weight)
        total = part if total is None else total + part
    return total


def fold(pieces, residue, blocks):
    cosines, sines = phases(residue, blocks)
    return weighted(pieces, cosines), weighted(pieces, sines)


def combine(spectrum, block, sub, first):
    cos_part = spectrum[:, :block]
    sin_part = spectrum[:, block:]
    fc, ic, uc = (cos_part[at * sub : (at + 1) * sub] for at in range(3))
    fs, i_s, us = (sin_part[at * sub : (at + 1) * sub] for at in range(3))
    cc = [fc * ic, fc * uc, uc * ic]
    ss = [fs * i_s, fs * us, us * i_s]
    new_cos = [cc[0] - ss[0], cc[1] + ss[1], cc[2] + ss[2]]
    new_sin = [fc * i_s + fs * ic, fc * us - fs * uc, us * ic - uc * i_s]
    new_cos = jnp.concatenate(new_cos, axis=0)
    new_sin = jnp.concatenate(new_sin, axis=0)
    if first:
        lane = lax.broadcasted_iota(jnp.int32, new_cos.shape, 1) == 0
        new_cos = jnp.where(lane, 0.5 * jnp.concatenate(cc, axis=0), new_cos)
        new_sin = jnp.where(lane, 0.5 * jnp.concatenate(ss, axis=0), new_sin)
    return jnp.concatenate([new_cos, new_sin], axis=1)


def convolve(pieces, high_ref, low_ref, turn_ref, sub):
    blocks = len(pieces)
    block = pieces[0].shape[1]
    rows = 3 * sub
    scale = 1.0 / (blocks * block)
    turns = [(turn_ref[at : at + 1], turn_ref[blocks + at : blocks + at + 1]) for at in range(blocks)]
    first = dot_both(jnp.concatenate(fold(pieces, 0, blocks), axis=1), high_ref[0], low_ref[0])
    packed = []
    for residue in range(1, blocks):
        even, odd = fold(pieces, residue, blocks)
        cosine, sine = turns[residue]
        packed.append(
            jnp.concatenate([even * cosine - odd * sine, even * sine + odd * cosine], axis=1)
        )
    spectrum = dot_both(jnp.concatenate(packed, axis=0), high_ref[1], low_ref[1])
    joined = [
        combine(spectrum[at * rows : (at + 1) * rows], block, sub, False) * scale
        for at in range(blocks - 1)
    ]
    head = dot_both(combine(first, block, sub, True) * scale, high_ref[0], low_ref[0], NT)
    back = dot_both(jnp.concatenate(joined, axis=0), high_ref[1], low_ref[1], NT)
    cosines, sines = phases(0, blocks)
    results = [
        weighted([head[:, :block], head[:, block:]], [cosines[at], sines[at]])
        for at in range(blocks)
    ]
    for residue in range(1, blocks):
        real = back[(residue - 1) * rows : residue * rows, :block]
        imag = back[(residue - 1) * rows : residue * rows, block:]
        cosine, sine = turns[residue]
        cosines, sines = phases(residue, blocks)
        pair = [real * cosine + imag * sine, imag * cosine - real * sine]
        for at in range(blocks):
            results[at] = results[at] + weighted(pair, [cosines[at], sines[at]])
    return results


def greet(devices, count):
    me = lax.axis_index("seq")
    spot = lax.axis_index("red")
    barrier = pltpu.get_barrier_semaphore()
    for step in range(1, devices):
        peer = lax.rem(me + step, devices)
        pl.semaphore_signal(barrier, inc=1, device_id={"seq": peer}, device_id_type=MESH)

    @pl.when(spot > 0)
    def _():
        pl.semaphore_signal(barrier, inc=1, device_id={"red": spot - 1}, device_id_type=MESH)

    @pl.when(spot < count - 1)
    def _():
        pl.semaphore_signal(barrier, inc=1, device_id={"red": spot + 1}, device_id_type=MESH)


def meet(devices, count):
    spot = lax.axis_index("red")
    neighbours = jnp.where(spot > 0, 1, 0) + jnp.where(spot < count - 1, 1, 0)
    pl.semaphore_wait(pltpu.get_barrier_semaphore(), devices - 1 + neighbours)


def exchange(devices, source, target, send_sem, recv_sem, base):
    me = lax.axis_index("seq")
    copies = []
    for step in range(1, devices):
        peer = lax.rem(me + step, devices)
        copy = pltpu.make_async_remote_copy(
            src_ref=source(peer),
            dst_ref=target(me),
            send_sem=send_sem.at[base + step - 1],
            recv_sem=recv_sem.at[base + step - 1],
            device_id={"seq": peer},
            device_id_type=MESH,
        )
        copy.start()
        copies.append(copy)
    return copies


def chunk_sizes(piece):
    return [piece * share // sum(SHARES) for share in SHARES]


def main_kernel(
    devices, count, scale_factor,
    tok_hbm, emb_hbm, wt_hbm, filt_hbm, cot_hbm, high_hbm, low_hbm, turn_hbm,
    out_ref, fgrad_ref, grads_ref, weight_ref,
    tok_ref, emb_ref, wt_ref, filt_ref, cot_ref, high_ref, low_ref, turn_ref,
    part, from_left, from_right, all_ref, out_sig, sig, sending, recv, one_hot,
    load_sem, wt_sem, sig_send, sig_recv, res_send, res_recv,
    right_send, right_recv, left_send, left_recv,
    up_send, up_recv, down_send, down_recv,
):
    me = lax.axis_index("seq")
    spot = lax.axis_index("red")
    branches, _, piece, _ = wt_ref.shape
    tok_count, width = filt_ref.shape
    vocabulary = emb_ref.shape[0]
    sizes = chunk_sizes(piece)
    starts = [sum(sizes[:at]) for at in range(len(sizes))]
    chunks = len(sizes)
    last = count - 1
    greet(devices, count)

    def goal_at(index):
        return jnp.where(spot * 2 < count, last - index, index)

    def load(index, source, target):
        copy = pltpu.make_async_copy(source, target, load_sem.at[index])
        copy.start()
        return copy

    emb_load = load(0, emb_hbm, emb_ref)
    wt_loads = []
    for index in range(count):
        goal = goal_at(index)
        copy = pltpu.make_async_copy(wt_hbm.at[:, goal], wt_ref.at[:, goal], wt_sem.at[index])
        copy.start()
        wt_loads.append(copy)
    signal_loads = [
        load(1, filt_hbm, filt_ref), load(2, cot_hbm, cot_ref), load(3, tok_hbm, tok_ref),
    ]
    table_loads = [
        load(4, high_hbm, high_ref), load(5, low_hbm, low_ref), load(6, turn_hbm, turn_ref),
    ]
    above_spot = jnp.minimum(spot + 1, last)
    below_spot = jnp.maximum(spot - 1, 0)

    def view(ref, chunk, group):
        return ref.at[group, pl.ds(branches * starts[chunk], branches * sizes[chunk])]

    def hop(source, target, chunk, group, sends, recvs, neighbour):
        slot = chunk * count + group
        return pltpu.make_async_remote_copy(
            src_ref=view(source, chunk, group),
            dst_ref=view(target, chunk, group),
            send_sem=sends.at[slot],
            recv_sem=recvs.at[slot],
            device_id={"red": neighbour},
            device_id_type=MESH,
        )

    def right(chunk, group):
        return hop(part, from_left, chunk, group, right_send, right_recv, above_spot)

    def left(chunk, group):
        return hop(part, from_right, chunk, group, left_send, left_recv, below_spot)

    def up(chunk, group):
        return hop(all_ref, all_ref, chunk, group, up_send, up_recv, above_spot)

    def down(chunk, group):
        return hop(all_ref, all_ref, chunk, group, down_send, down_recv, below_spot)

    def add(target, source, chunk, group):
        view(target, chunk, group)[...] = view(target, chunk, group)[...] + view(source, chunk, group)[...]

    def products(index):
        goal = goal_at(index)
        wt_loads[index].wait()
        rows = jnp.concatenate([wt_ref[b, goal] for b in range(branches)], axis=0)
        product = dot(rows, emb_ref[...], NT)
        for start, size in zip(starts, sizes):
            for b in range(branches):
                base = branches * start + b * size
                part[goal, base : base + size] = product[b * piece + start : b * piece + start + size]

    def first_hop(chunk, index):
        @pl.when(spot == 0)
        def _():
            right(chunk, last - index).start()

        @pl.when(spot == last)
        def _():
            left(chunk, index).start()

    def middle_hops(chunk):
        for tick in range(1, last):
            goal = last - (tick - spot)

            @pl.when((spot > 0) & (tick >= spot) & (spot < goal))
            def _():
                right(chunk, goal).wait_recv()
                add(part, from_left, chunk, goal)
                right(chunk, goal).start()

            other = tick - (last - spot)

            @pl.when((spot < last) & (other >= 0) & (spot > other))
            def _():
                left(chunk, other).wait_recv()
                add(part, from_right, chunk, other)
                left(chunk, other).start()

    def arrive(chunk):
        @pl.when(spot > 0)
        def _():
            right(chunk, spot).wait_recv()
            add(part, from_left, chunk, spot)

        @pl.when(spot < last)
        def _():
            left(chunk, spot).wait_recv()
            add(part, from_right, chunk, spot)

        return view(part, chunk, spot)[...]

    def share(chunk):
        @pl.when(spot < last)
        def _():
            up(chunk, spot).start()

        @pl.when(spot > 0)
        def _():
            down(chunk, spot).start()

    def relay(chunk, sources, distance):
        for source in sources:
            if source < last:
                @pl.when((spot < last) & (spot - source == distance))
                def _():
                    up(chunk, source).wait_recv()
                    up(chunk, source).start()

            if source > 0:
                @pl.when((spot > 0) & (source - spot == distance))
                def _():
                    down(chunk, source).wait_recv()
                    down(chunk, source).start()

    inner = list(range(1, last))
    ends = [0, last]

    def relay_far(chunk):
        for distance in range(2, last):
            relay(chunk, range(count), distance)

    def collect(chunk):
        for step in range(1, count):
            @pl.when(spot == 0)
            def _():
                down(chunk, step).wait_recv()

            @pl.when(spot == last)
            def _():
                up(chunk, last - step).wait_recv()

    def weights(chunk):
        start, size = starts[chunk], sizes[chunk]
        blocks = jnp.concatenate([view(all_ref, chunk, group)[...] for group in range(count)], axis=0)
        product = dot_split(blocks, emb_ref[...]) * scale_factor
        for group in range(count):
            for b in range(branches):
                base = (group * branches + b) * size
                weight_ref[b, group, start : start + size] = product[base : base + size]

    def signal_rows(start, rows, at):
        return sig[at, start : start + rows]

    def channels(chunk, own):
        start, size = starts[chunk], sizes[chunk]
        projected = dot_split(own, one_hot[...])
        pieces = []
        held = []
        for at in range(devices):
            block = projected[:, at * tok_count : (at + 1) * tok_count]
            queries, key_rows, value_rows = (block[b * size : (b + 1) * size] for b in range(3))
            cotangent = signal_rows(piece + start, size, at)
            held.append((queries, key_rows, value_rows, cotangent))
            pieces.append(
                jnp.concatenate(
                    [signal_rows(start, size, at), key_rows * value_rows, cotangent * queries], axis=0
                )
            )
        results = convolve(pieces, high_ref, low_ref, turn_ref, size)
        rounded = []
        for at in range(devices):
            queries, key_rows, value_rows, cotangent = held[at]
            conv = results[at][:size]
            grad_inner = results[at][size : 2 * size]
            grads = jnp.concatenate(
                [cotangent * conv, grad_inner * value_rows, grad_inner * key_rows], axis=0
            ).astype(jnp.bfloat16)
            rounded.append(grads)
            base = 5 * start
            sending[at, base : base + size] = queries * conv
            sending[at, base + size : base + 2 * size] = results[at][2 * size :] * scale_factor
            sending[at, base + 2 * size : base + 5 * size] = grads.astype(jnp.float32)
        sums = dot(jnp.concatenate(rounded, axis=1), one_hot[...], NT)
        view(all_ref, chunk, spot)[...] = sums

    def positions(at):
        parts = [
            recv[peer, 5 * start + at * size : 5 * start + (at + 1) * size]
            for peer in range(devices)
            for start, size in zip(starts, sizes)
        ]
        return jnp.concatenate(parts, axis=0).T

    emb_load.wait()
    products(0)
    meet(devices, count)
    first_hop(0, 0)
    for copy in signal_loads:
        copy.wait()
    filt_t = filt_ref[...].T
    cot_t = cot_ref[...].T
    tok_rows = jnp.broadcast_to(tok_ref[...].astype(jnp.float32), (8, tok_count))
    for peer in range(devices):
        out_sig[peer, :piece] = filt_t[peer * piece : (peer + 1) * piece]
        out_sig[peer, piece : 2 * piece] = cot_t[peer * piece : (peer + 1) * piece]
        out_sig[peer, 2 * piece :] = tok_rows
    copies = exchange(devices, out_sig.at.__getitem__, sig.at.__getitem__, sig_send, sig_recv, 0)
    for index in range(1, count):
        products(index)
        if index < last:
            first_hop(0, index)
    for chunk in range(1, chunks):
        for index in range(last):
            first_hop(chunk, index)
    sig[me] = out_sig[me]
    sent = list(copies)
    arrivals = []
    for chunk in range(chunks):
        middle_hops(chunk)
        if chunk > 0:
            relay(chunk - 1, inner, 1)
        else:
            for copy in copies:
                copy.wait_recv()
            ids = jnp.concatenate([signal_rows(2 * piece, 1, at) for at in range(devices)], axis=1)
            vocab_rows = lax.broadcasted_iota(jnp.int32, (vocabulary, devices * tok_count), 0)
            one_hot[...] = jnp.where(vocab_rows == ids.astype(jnp.int32), 1.0, 0.0).astype(jnp.bfloat16)
            for copy in table_loads:
                copy.wait()
        channels(chunk, arrive(chunk))
        share(chunk)
        rows = pl.ds(5 * starts[chunk], 5 * sizes[chunk])
        more = exchange(
            devices,
            lambda peer, rows=rows: sending.at[peer, rows],
            lambda slot, rows=rows: recv.at[slot, rows],
            res_send, res_recv, chunk * (devices - 1),
        )
        recv[me, 5 * starts[chunk] : 5 * (starts[chunk] + sizes[chunk])] = sending[
            me, 5 * starts[chunk] : 5 * (starts[chunk] + sizes[chunk])
        ]
        sent += more
        arrivals += more
    final = chunks - 1
    for chunk in range(final):
        relay(chunk, ends, 1)
    relay(final, inner, 1)
    for chunk in range(final):
        relay_far(chunk)
    for chunk in range(final):
        collect(chunk)
        weights(chunk)
    relay(final, ends, 1)
    for copy in arrivals:
        copy.wait_recv()
    out_ref[...] = positions(0)
    fgrad_ref[...] = positions(1)
    for branch in range(branches):
        grads_ref[branch] = positions(2 + branch).astype(jnp.bfloat16)
    relay_far(final)
    collect(final)
    weights(final)
    for chunk in range(chunks):
        for group in range(count):
            @pl.when(spot < group)
            def _():
                right(chunk, group).wait_send()

            @pl.when(spot > group)
            def _():
                left(chunk, group).wait_send()

            @pl.when((spot >= group) & (spot < last))
            def _():
                up(chunk, group).wait_send()

            @pl.when((spot <= group) & (spot > 0))
            def _():
                down(chunk, group).wait_send()

    for copy in sent:
        copy.wait_send()


def final_kernel(out_in, fgrad_in, grads_in, weight_in, out_ref, fgrad_ref, grads_ref, weight_ref, sem):
    pairs = [(weight_in, weight_ref), (grads_in, grads_ref), (out_in, out_ref), (fgrad_in, fgrad_ref)]
    copies = [
        pltpu.make_async_copy(source, target, sem.at[index])
        for index, (source, target) in enumerate(pairs)
    ]
    for copy in copies:
        copy.start()
    for copy in copies:
        copy.wait()


def kernel_shards(devices, count, token_ids, embedding, proj_weight, filters, cotangent):
    tok_count, width = filters.shape
    vocabulary, depth = embedding.shape
    _, branches, _, piece = proj_weight.shape
    scale_factor = float(tok_count * devices) ** (-0.5)
    chunks = len(SHARES)
    f32 = jnp.float32
    bf16 = jnp.bfloat16
    dma = pltpu.SemaphoreType.DMA
    weight_t = jnp.transpose(proj_weight, (1, 2, 3, 0))
    high, low, turn = transform_tables(tok_count, devices)
    block = (count, branches * piece, vocabulary)
    message = (devices, 2 * piece + 8, tok_count)
    answer = (devices, 5 * piece, tok_count)
    results = (
        ((tok_count, width), f32),
        ((tok_count, width), f32),
        ((branches, tok_count, width), bf16),
        ((branches, count, piece, depth), f32),
    )
    kept = sum(math.prod(shape) * jnp.dtype(kind).itemsize for shape, kind in results) + 2**17
    held = pl.pallas_call(
        functools.partial(main_kernel, devices, count, scale_factor),
        out_shape=tuple(pltpu.VMEM(shape, kind) for shape, kind in results),
        in_specs=[pl.BlockSpec(memory_space=pltpu.HBM)] * 8,
        out_specs=(VMEM,) * 4,
        scratch_shapes=[
            pltpu.VMEM((1, tok_count), jnp.int32),
            pltpu.VMEM(embedding.shape, bf16),
            pltpu.VMEM(weight_t.shape, bf16),
            pltpu.VMEM(filters.shape, f32),
            pltpu.VMEM(cotangent.shape, f32),
            pltpu.VMEM(high.shape, bf16),
            pltpu.VMEM(low.shape, bf16),
            pltpu.VMEM(turn.shape, f32),
            pltpu.VMEM(block, f32),
            pltpu.VMEM(block, f32),
            pltpu.VMEM(block, f32),
            pltpu.VMEM(block, f32),
            pltpu.VMEM(message, f32),
            pltpu.VMEM(message, f32),
            pltpu.VMEM(answer, f32),
            pltpu.VMEM(answer, f32),
            pltpu.VMEM((vocabulary, devices * tok_count), bf16),
            dma((7,)),
            dma((count,)),
            dma((devices - 1,)),
            dma((devices - 1,)),
            dma((chunks * (devices - 1),)),
            dma((chunks * (devices - 1),)),
        ]
        + [dma((chunks * count,))] * 8,
        compiler_params=pltpu.CompilerParams(
            collective_id=0, has_side_effects=True, vmem_limit_bytes=VMEM_BYTES - kept
        ),
        name="hyena_exchange",
    )(
        token_ids.reshape(1, tok_count), embedding, weight_t, filters, cotangent,
        jnp.asarray(high), jnp.asarray(low), jnp.asarray(turn),
    )
    output, filter_grad, grads, weight = pl.pallas_call(
        final_kernel,
        out_shape=tuple(jax.ShapeDtypeStruct(shape, kind) for shape, kind in results),
        in_specs=[VMEM] * 4,
        out_specs=(pl.BlockSpec(memory_space=pltpu.HBM),) * 4,
        scratch_shapes=[dma((4,))],
        compiler_params=pltpu.CompilerParams(vmem_limit_bytes=2**20),
        name="finish",
    )(*held)
    return (
        output,
        filter_grad,
        jnp.transpose(grads, (1, 0, 2)),
        jnp.transpose(weight, (3, 0, 1, 2)),
    )


def fits_kernels(devices, count, token_ids, embedding, proj_weight, filters):
    tok_count, width = filters.shape
    vocabulary, depth = embedding.shape
    _, branches, red_count, piece = proj_weight.shape
    lanes = (tok_count, vocabulary, depth)
    aligned = all(size % 128 == 0 for size in lanes) and piece % (8 * sum(SHARES)) == 0
    one_hot = vocabulary * tok_count * devices * 8
    held = 4 * branches * piece * (4 * count * vocabulary + 2 * count * depth)
    sides = 4 * tok_count * devices * 20 * piece + 16 * vocabulary * depth
    return (
        aligned
        and count > 1
        and branches == 3
        and red_count == count
        and width == devices * piece
        and one_hot + held + sides < 36 * 2**20
    )


def angles(numbers, modulus, direction):
    phase = (numbers % modulus).astype(jnp.float32) * (direction * 2.0 * math.pi / modulus)
    return (jnp.cos(phase), jnp.sin(phase))


def rotate(real_part, imag_part, cosine, sine_part):
    return (real_part * cosine - imag_part * sine_part, real_part * sine_part + imag_part * cosine)


def complex_einsum(formula, matrix, values):
    mat_real, mat_imag = matrix
    val_real, val_imag = values
    real_out = jnp.einsum(formula, mat_real, val_real, precision=precise_mode) - jnp.einsum(
        formula, mat_imag, val_imag, precision=precise_mode
    )
    imag_out = jnp.einsum(formula, mat_real, val_imag, precision=precise_mode) + jnp.einsum(
        formula, mat_imag, val_real, precision=precise_mode
    )
    return (real_out, imag_out)


def factors(length_total):
    first_factor = 1
    for candidate in range(1, math.isqrt(length_total) + 1):
        if length_total % candidate == 0:
            first_factor = candidate
    return (first_factor, length_total // first_factor)


def combine_spectra(spec_real, spec_imag, width):
    filt_re = spec_real[..., :width]
    inner_re = spec_real[..., width : 2 * width]
    up_re = spec_real[..., 2 * width :]
    filt_im = spec_imag[..., :width]
    inner_im = spec_imag[..., width : 2 * width]
    up_im = spec_imag[..., 2 * width :]
    joined_real = jnp.concatenate(
        [
            filt_re * inner_re - filt_im * inner_im,
            filt_re * up_re + filt_im * up_im,
            up_re * inner_re + up_im * inner_im,
        ],
        axis=-1,
    )
    joined_imag = jnp.concatenate(
        [
            filt_re * inner_im + filt_im * inner_re,
            filt_re * up_im - filt_im * up_re,
            up_im * inner_re - up_re * inner_im,
        ],
        axis=-1,
    )
    return (joined_real, joined_imag)


def local_convolve(signals):
    length, branch_count, narrow = signals.shape
    total = 2 * length
    first_factor, second_factor = factors(total)
    flat = signals.reshape(length, branch_count * narrow)
    padded = jnp.concatenate([flat, jnp.zeros_like(flat)], axis=0).reshape(
        first_factor, second_factor, branch_count * narrow
    )
    first_index = jnp.arange(first_factor, dtype=jnp.int32)
    second_index = jnp.arange(second_factor, dtype=jnp.int32)
    cosine, sine_part = angles(first_index[:, None] * first_index[None, :], first_factor, -1.0)
    real_part = jnp.einsum("kn,nbm->kbm", cosine, padded, precision=precise_mode)
    imag_part = jnp.einsum("kn,nbm->kbm", sine_part, padded, precision=precise_mode)
    cosine, sine_part = angles(first_index[:, None] * second_index[None, :], total, -1.0)
    real_part, imag_part = rotate(real_part, imag_part, cosine[:, :, None], sine_part[:, :, None])
    real_part, imag_part = complex_einsum(
        "lb,kbm->klm",
        angles(second_index[:, None] * second_index[None, :], second_factor, -1.0),
        (real_part, imag_part),
    )
    real_part, imag_part = combine_spectra(real_part, imag_part, narrow)
    real_part, imag_part = complex_einsum(
        "bl,klm->kbm",
        angles(second_index[:, None] * second_index[None, :], second_factor, 1.0),
        (real_part, imag_part),
    )
    cosine, sine_part = angles(first_index[:, None] * second_index[None, :], total, 1.0)
    real_part, imag_part = rotate(real_part, imag_part, cosine[:, :, None], sine_part[:, :, None])
    cosine, sine_part = angles(first_index[:, None] * first_index[None, :], first_factor, 1.0)
    result = jnp.einsum("nk,kbm->nbm", cosine, real_part, precision=precise_mode) - jnp.einsum(
        "nk,kbm->nbm", sine_part, imag_part, precision=precise_mode
    )
    result = result.reshape(total, branch_count * narrow)[:length] / total
    return result.reshape(length, branch_count, narrow)


def shards(token_ids, embedding, proj_weight, filters, cotangent):
    tok_count = token_ids.shape[0]
    devices = lax.axis_size("seq")
    count = lax.axis_size("red")
    if fits_kernels(devices, count, token_ids, embedding, proj_weight, filters):
        return kernel_shards(
            devices, count, token_ids, embedding, proj_weight, filters, cotangent
        )
    width = filters.shape[1]
    vocabulary = embedding.shape[0]
    width_rows, branches, red_count, piece = proj_weight.shape
    scale_factor = float(tok_count * devices) ** (-0.5)
    table = jnp.dot(
        embedding,
        proj_weight.reshape(width_rows, branches * red_count * piece),
        preferred_element_type=jnp.float32,
    )
    table = table.reshape(vocabulary, branches, red_count, piece)
    own_table = lax.psum_scatter(table, "red", scatter_dimension=2, tiled=True)
    full_table = lax.all_gather(own_table, "seq", axis=3, tiled=True)
    projected = jnp.take(full_table, token_ids, axis=0)
    projected = projected.reshape(tok_count, branches, width)
    queries = projected[:, 0]
    key_rows = projected[:, 1]
    value_rows = projected[:, 2]
    inner = key_rows * value_rows
    upstream = cotangent * queries
    stacked = jnp.stack([filters, inner, upstream], axis=1)
    whole_length = lax.all_to_all(stacked, "seq", split_axis=2, concat_axis=0, tiled=True)
    results = local_convolve(whole_length)
    returned = lax.all_to_all(results, "seq", split_axis=0, concat_axis=2, tiled=True)
    conv = returned[:, 0]
    grad_inner = returned[:, 1]
    filter_raw = returned[:, 2]
    output = queries * conv
    filter_grad = filter_raw * scale_factor
    branch_grads = jnp.stack(
        [cotangent * conv, grad_inner * value_rows, grad_inner * key_rows], axis=1
    ).astype(jnp.bfloat16)
    one_hot = (token_ids[:, None] == lax.iota(jnp.int32, vocabulary)[None, :]).astype(jnp.bfloat16)
    token_sums = lax.dot_general(
        one_hot,
        branch_grads.reshape(tok_count, branches * width),
        (((0,), (0,)), ((), ())),
        preferred_element_type=jnp.float32,
    )
    summed = lax.psum_scatter(
        token_sums.reshape(vocabulary, branches, width), "seq", scatter_dimension=2, tiled=True
    )
    gathered = lax.all_gather(summed[:, :, None, :], "red", axis=2, tiled=True)
    weight_grad = (
        lax.dot_general(
            embedding.astype(jnp.float32),
            gathered.reshape(vocabulary, branches * red_count * piece),
            (((0,), (0,)), ((), ())),
            precision=precise_mode,
        )
        * scale_factor
    )
    return (
        output,
        filter_grad,
        branch_grads,
        weight_grad.reshape(width_rows, branches, red_count, piece),
    )


def solution(mesh):
    in_specs = (
        P("seq"),
        P(None, "red"),
        P("red", None, None, "seq"),
        P("seq", "red"),
        P("seq", "red"),
    )
    out_specs = (
        P("seq", "red"),
        P("seq", "red"),
        P("seq", None, "red"),
        P("red", None, None, "seq"),
    )
    return jax.shard_map(shards, mesh=mesh, in_specs=in_specs, out_specs=out_specs, check_vma=False)
```

time: 45.5 us -> 41.6 us (0.914)
  Pallas kernels: 44.7 us -> 40.8 us
    pallas_call x2, Pallas kernels: 44.7 us -> 40.8 us  [the longest x1 39.4 us: kernel_shards(): pl.pallas_call(functools.partial(main_kernel, devices, count, scale_facto...]
where the time goes in v1:
time: 41.6 us; the launch traced here: 41.4 us
  Pallas kernels  40.8 us (98%)
  between operations  0.64 us (2%)
    pallas_call x1, Pallas kernels, kernel_shards(): pl.pallas_call(functools.partial(main_kernel, devices, count, scale_facto...  39.4 us
    pallas_call x1, Pallas kernels, kernel_shards(): pl.pallas_call(final_kernel, out_shape=tuple((jax.ShapeDtypeStruct(shape,...  1.32 us

profile of v1, /device:TPU:0, one launch (start us, length us, event | category | flops | bytes accessed | tf_op | source)
XLA Modules:
  0.0 41.4 jit_solution(4156258664314684094)
XLA Ops:
  0.6 39.4 %hyena_exchange.1 = (f32[128,256]{1,0:T(8,128)S(1)}, f32[128,256]{1,0:T(8,128)S(1)}, bf16[3,128,256]{2,1,0:T(8,128)(2,1)S(1)}, f32[3,4,32,1024]{3,2,1,0:T(8,128)S(1)}) custom-call(s32[1,128]{1,0:T(1,128)} %bitcast.5, bf16[512,1024]{1,0:T(8,128)(2,1)} %emb_hbm.1, bf16[3,4,32,1024]{3,2,1,0:T(8,128)(2,1)} %bitcast.4, f32[128,256]{1,0:T(8,128)} %filt_hbm.1, ...), custom_call_target="tpu_custom_call" | custom-call | tf_op jit(solution)/shard_map/hyena_exchange/pallas_call | solution.py:527
  40.1 1.3 %finish.1 = (f32[128,256]{1,0:T(8,128)}, f32[128,256]{1,0:T(8,128)}, bf16[3,128,256]{2,1,0:T(8,128)(2,1)}, f32[3,4,32,1024]{3,2,1,0:T(8,128)}) custom-call(f32[128,256]{1,0:T(8,128)S(1)} %get-tuple-element.12.out_in, f32[128,256]{1,0:T(8,128)S(1)} %get-tuple-element.13.fgrad_in, bf16[3,128,256]{2,1,0:T(8,128)(2,1)S(1)} %get-tuple-element.14.grads_in, ...), custom_call_target="tpu_custom_call" | custom-call | tf_op jit(solution)/shard_map/finish/pallas_call | solution.py:566

commit v2 on v1

--- a/solution.py
+++ b/solution.py
@@ -13,6 +13,7 @@
 MESH = pl.DeviceIdType.MESH
 VMEM = pl.BlockSpec(memory_space=pltpu.VMEM)
 SHARES = (1,)
+PIECES = 4
 VMEM_BYTES = 67043328
 NN = (((1,), (0,)), ((), ()))
 NT = (((1,), (1,)), ((), ()))
@@ -229,34 +230,40 @@
     above_spot = jnp.minimum(spot + 1, last)
     below_spot = jnp.maximum(spot - 1, 0)
 
-    def view(ref, chunk, group):
-        return ref.at[group, pl.ds(branches * starts[chunk], branches * sizes[chunk])]
-
-    def hop(source, target, chunk, group, sends, recvs, neighbour):
-        slot = chunk * count + group
+    def view(ref, chunk, group, at=None):
+        rows = branches * sizes[chunk]
+        base = branches * starts[chunk]
+        if at is not None:
+            rows //= PIECES
+            base += at * rows
+        return ref.at[group, pl.ds(base, rows)]
+
+    def hop(source, target, chunk, group, at, sends, recvs, neighbour):
+        slot = (chunk * count + group) * PIECES + at
         return pltpu.make_async_remote_copy(
-            src_ref=view(source, chunk, group),
-            dst_ref=view(target, chunk, group),
+            src_ref=view(source, chunk, group, at),
+            dst_ref=view(target, chunk, group, at),
             send_sem=sends.at[slot],
             recv_sem=recvs.at[slot],
             device_id={"red": neighbour},
             device_id_type=MESH,
         )
 
-    def right(chunk, group):
-        return hop(part, from_left, chunk, group, right_send, right_recv, above_spot)
-
-    def left(chunk, group):
-        return hop(part, from_right, chunk, group, left_send, left_recv, below_spot)
-
-    def up(chunk, group):
-        return hop(all_ref, all_ref, chunk, group, up_send, up_recv, above_spot)
-
-    def down(chunk, group):
-        return hop(all_ref, all_ref, chunk, group, down_send, down_recv, below_spot)
-
-    def add(target, source, chunk, group):
-        view(target, chunk, group)[...] = view(target, chunk, group)[...] + view(source, chunk, group)[...]
+    def right(chunk, group, at):
+        return hop(part, from_left, chunk, group, at, right_send, right_recv, above_spot)
+
+    def left(chunk, group, at):
+        return hop(part, from_right, chunk, group, at, left_send, left_recv, below_spot)
+
+    def up(chunk, group, at):
+        return hop(all_ref, all_ref, chunk, group, at, up_send, up_recv, above_spot)
+
+    def down(chunk, group, at):
+        return hop(all_ref, all_ref, chunk, group, at, down_send, down_recv, below_spot)
+
+    def add(target, source, chunk, group, at):
+        piece_ref = view(target, chunk, group, at)
+        piece_ref[...] = piece_ref[...] + view(source, chunk, group, at)[...]
 
     def products(index):
         goal = goal_at(index)
@@ -271,91 +278,94 @@
     def first_hop(chunk, index):
         @pl.when(spot == 0)
         def _():
-            right(chunk, last - index).start()
+            for at in range(PIECES):
+                right(chunk, last - index, at).start()
 
         @pl.when(spot == last)
         def _():
-            left(chunk, index).start()
+            for at in range(PIECES):
+                left(chunk, index, at).start()
 
     def middle_hops(chunk):
         for tick in range(1, last):
-            goal = last - (tick - spot)
-
-            @pl.when((spot > 0) & (tick >= spot) & (spot < goal))
+            for at in range(PIECES):
+                goal = last - (tick - spot)
+
+                @pl.when((spot > 0) & (tick >= spot) & (spot < goal))
+                def _():
+                    right(chunk, goal, at).wait_recv()
+                    add(part, from_left, chunk, goal, at)
+                    right(chunk, goal, at).start()
+
+                other = tick - (last - spot)
+
+                @pl.when((spot < last) & (other >= 0) & (spot > other))
+                def _():
+                    left(chunk, other, at).wait_recv()
+                    add(part, from_right, chunk, other, at)
+                    left(chunk, other, at).start()
+
+    def arrive(chunk):
+        for at in range(PIECES):
+            @pl.when(spot > 0)
             def _():
-                right(chunk, goal).wait_recv()
-                add(part, from_left, chunk, goal)
-                right(chunk, goal).start()
-
-            other = tick - (last - spot)
-
-            @pl.when((spot < last) & (other >= 0) & (spot > other))
+                right(chunk, spot, at).wait_recv()
+                add(part, from_left, chunk, spot, at)
+
+            @pl.when(spot < last)
             def _():
-                left(chunk, other).wait_recv()
-                add(part, from_right, chunk, other)
-                left(chunk, other).start()
-
-    def arrive(chunk):
-        @pl.when(spot > 0)
-        def _():
-            right(chunk, spot).wait_recv()
-            add(part, from_left, chunk, spot)
-
-        @pl.when(spot < last)
-        def _():
-            left(chunk, spot).wait_recv()
-            add(part, from_right, chunk, spot)
+                left(chunk, spot, at).wait_recv()
+                add(part, from_right, chunk, spot, at)
 
         return view(part, chunk, spot)[...]
 
     def share(chunk):
-        @pl.when(spot < last)
-        def _():
-            up(chunk, spot).start()
-
-        @pl.when(spot > 0)
-        def _():
-            down(chunk, spot).start()
-
-    def relay(chunk, sources, distance):
-        for source in sources:
-            if source < last:
-                @pl.when((spot < last) & (spot - source == distance))
-                def _():
-                    up(chunk, source).wait_recv()
-                    up(chunk, source).start()
-
-            if source > 0:
-                @pl.when((spot > 0) & (source - spot == distance))
-                def _():
-                    down(chunk, source).wait_recv()
-                    down(chunk, source).start()
-
-    inner = list(range(1, last))
-    ends = [0, last]
-
-    def relay_far(chunk):
-        for distance in range(2, last):
-            relay(chunk, range(count), distance)
-
-    def collect(chunk):
-        for step in range(1, count):
+        for at in range(PIECES):
+            @pl.when(spot < last)
+            def _():
+                up(chunk, spot, at).start()
+
+            @pl.when(spot > 0)
+            def _():
+                down(chunk, spot, at).start()
+
+    def relay(chunk, step):
+        below = spot - step
+        above = spot + step
+        for at in range(PIECES):
+            @pl.when((below >= 0) & (spot < last))
+            def _():
+                up(chunk, below, at).wait_recv()
+                up(chunk, below, at).start()
+
+            @pl.when((above < count) & (spot > 0))
+            def _():
+                down(chunk, above, at).wait_recv()
+                down(chunk, above, at).start()
+
+    def nearest(step):
+        group = 0
+        for place in range(count):
+            order = sorted(range(count), key=lambda other: (abs(other - place), abs(2 * other - last)))
+            group = jnp.where(spot == place, order[step], group)
+        return group
+
+    def collect(chunk, step):
+        for at in range(PIECES):
             @pl.when(spot == 0)
             def _():
-                down(chunk, step).wait_recv()
+                down(chunk, step, at).wait_recv()
 
             @pl.when(spot == last)
             def _():
-                up(chunk, last - step).wait_recv()
-
-    def weights(chunk):
+                up(chunk, last - step, at).wait_recv()
+
+    def weights(chunk, step):
         start, size = starts[chunk], sizes[chunk]
-        blocks = jnp.concatenate([view(all_ref, chunk, group)[...] for group in range(count)], axis=0)
-        product = dot_split(blocks, emb_ref[...]) * scale_factor
-        for group in range(count):
-            for b in range(branches):
-                base = (group * branches + b) * size
-                weight_ref[b, group, start : start + size] = product[base : base + size]
+        group = nearest(step)
+        product = dot_split(view(all_ref, chunk, group)[...], emb_ref[...]) * scale_factor
+        for b in range(branches):
+            weight_ref[b, group, start : start + size] = product[b * size : (b + 1) * size]
 
     def signal_rows(start, rows, at):
         return sig[at, start : start + rows]
@@ -426,9 +436,7 @@
     arrivals = []
     for chunk in range(chunks):
         middle_hops(chunk)
-        if chunk > 0:
-            relay(chunk - 1, inner, 1)
-        else:
+        if chunk == 0:
             for copy in copies:
                 copy.wait_recv()
             ids = jnp.concatenate([signal_rows(2 * piece, 1, at) for at in range(devices)], axis=1)
@@ -450,42 +458,39 @@
         ]
         sent += more
         arrivals += more
-    final = chunks - 1
-    for chunk in range(final):
-        relay(chunk, ends, 1)
-    relay(final, inner, 1)
-    for chunk in range(final):
-        relay_far(chunk)
-    for chunk in range(final):
-        collect(chunk)
-        weights(chunk)
-    relay(final, ends, 1)
-    for copy in arrivals:
-        copy.wait_recv()
-    out_ref[...] = positions(0)
-    fgrad_ref[...] = positions(1)
-    for branch in range(branches):
-        grads_ref[branch] = positions(2 + branch).astype(jnp.bfloat16)
-    relay_far(final)
-    collect(final)
-    weights(final)
+        weights(chunk, 0)
+    for chunk in range(chunks):
+        for step in range(1, last):
+            relay(chunk, step)
+    for step in range(1, count):
+        for chunk in range(chunks):
+            if step == last and chunk == chunks - 1:
+                for copy in arrivals:
+                    copy.wait_recv()
+                out_ref[...] = positions(0)
+                fgrad_ref[...] = positions(1)
+                for branch in range(branches):
+                    grads_ref[branch] = positions(2 + branch).astype(jnp.bfloat16)
+            collect(chunk, step)
+            weights(chunk, step)
     for chunk in range(chunks):
         for group in range(count):
-            @pl.when(spot < group)
-            def _():
-                right(chunk, group).wait_send()
-
-            @pl.when(spot > group)
-            def _():
-                left(chunk, group).wait_send()
-
-            @pl.when((spot >= group) & (spot < last))
-            def _():
-                up(chunk, group).wait_send()
-
-            @pl.when((spot <= group) & (spot > 0))
-            def _():
-                down(chunk, group).wait_send()
+            for at in range(PIECES):
+                @pl.when(spot < group)
+                def _():
+                    right(chunk, group, at).wait_send()
+
+                @pl.when(spot > group)
+                def _():
+                    left(chunk, group, at).wait_send()
+
+                @pl.when((spot >= group) & (spot < last))
+                def _():
+                    up(chunk, group, at).wait_send()
+
+                @pl.when((spot <= group) & (spot > 0))
+                def _():
+                    down(chunk, group, at).wait_send()
 
     for copy in sent:
         copy.wait_send()
@@ -554,7 +559,7 @@
             dma((chunks * (devices - 1),)),
             dma((chunks * (devices - 1),)),
         ]
-        + [dma((chunks * count,))] * 8,
+        + [dma((chunks * count * PIECES,))] * 8,
         compiler_params=pltpu.CompilerParams(
             collective_id=0, has_side_effects=True, vmem_limit_bytes=VMEM_BYTES - kept
         ),
@@ -585,7 +590,7 @@
     vocabulary, depth = embedding.shape
     _, branches, red_count, piece = proj_weight.shape
     lanes = (tok_count, vocabulary, depth)
-    aligned = all(size % 128 == 0 for size in lanes) and piece % (8 * sum(SHARES)) == 0
+    aligned = all(size % 128 == 0 for size in lanes) and piece % (8 * sum(SHARES)) == 0 and branches * piece % (8 * sum(SHARES) * PIECES) == 0
     one_hot = vocabulary * tok_count * devices * 8
     held = 4 * branches * piece * (4 * count * vocabulary + 2 * count * depth)
     sides = 4 * tok_count * devices * 20 * piece + 16 * vocabulary * depth

time: 41.6 us -> 39.6 us (0.952)
  Pallas kernels: 40.8 us -> 38.8 us
    pallas_call x1, Pallas kernels: 39.4 us -> 37.4 us  [kernel_shards(): pl.pallas_call(functools.partial(main_kernel, devices, count, scale_facto...]
where the time goes in v2:
time: 39.6 us; the launch traced here: 39.4 us
  Pallas kernels  38.8 us (98%)
  between operations  0.64 us (2%)
    pallas_call x1, Pallas kernels, kernel_shards(): pl.pallas_call(functools.partial(main_kernel, devices, count, scale_facto...  37.4 us
    pallas_call x1, Pallas kernels, kernel_shards(): pl.pallas_call(final_kernel, out_shape=tuple((jax.ShapeDtypeStruct(shape,...  1.32 us

profile of v2, /device:TPU:0, one launch (start us, length us, event | category | flops | bytes accessed | tf_op | source)
XLA Modules:
  0.0 39.4 jit_solution(14163135108771641158)
XLA Ops:
  0.6 37.4 %hyena_exchange.1 = (f32[128,256]{1,0:T(8,128)S(1)}, f32[128,256]{1,0:T(8,128)S(1)}, bf16[3,128,256]{2,1,0:T(8,128)(2,1)S(1)}, f32[3,4,32,1024]{3,2,1,0:T(8,128)S(1)}) custom-call(s32[1,128]{1,0:T(1,128)} %bitcast.5, bf16[512,1024]{1,0:T(8,128)(2,1)} %emb_hbm.1, bf16[3,4,32,1024]{3,2,1,0:T(8,128)(2,1)} %bitcast.4, f32[128,256]{1,0:T(8,128)} %filt_hbm.1, ...), custom_call_target="tpu_custom_call" | custom-call | tf_op jit(solution)/shard_map/hyena_exchange/pallas_call | solution.py:532
  38.1 1.3 %finish.1 = (f32[128,256]{1,0:T(8,128)}, f32[128,256]{1,0:T(8,128)}, bf16[3,128,256]{2,1,0:T(8,128)(2,1)}, f32[3,4,32,1024]{3,2,1,0:T(8,128)}) custom-call(f32[128,256]{1,0:T(8,128)S(1)} %get-tuple-element.12.out_in, f32[128,256]{1,0:T(8,128)S(1)} %get-tuple-element.13.fgrad_in, bf16[3,128,256]{2,1,0:T(8,128)(2,1)S(1)} %get-tuple-element.14.grads_in, ...), custom_call_target="tpu_custom_call" | custom-call | tf_op jit(solution)/shard_map/finish/pallas_call | solution.py:571

commit v3 on v1

--- a/solution.py
+++ b/solution.py
@@ -12,7 +12,9 @@
 precise_mode = lax.Precision.HIGHEST
 MESH = pl.DeviceIdType.MESH
 VMEM = pl.BlockSpec(memory_space=pltpu.VMEM)
-SHARES = (1,)
+SHARES = (1, 1)
+REDUCE_DIRECT = (False, True)
+PIECES = 3
 VMEM_BYTES = 67043328
 NN = (((1,), (0,)), ((), ()))
 NT = (((1,), (1,)), ((), ()))
@@ -139,45 +141,55 @@
     return results
 
 
+def partners(count):
+    spot = lax.axis_index("red")
+    return spot + 1 - 2 * lax.rem(spot, 2), count - 1 - spot
+
+
 def greet(devices, count):
     me = lax.axis_index("seq")
-    spot = lax.axis_index("red")
     barrier = pltpu.get_barrier_semaphore()
     for step in range(1, devices):
         peer = lax.rem(me + step, devices)
         pl.semaphore_signal(barrier, inc=1, device_id={"seq": peer}, device_id_type=MESH)
-
-    @pl.when(spot > 0)
-    def _():
-        pl.semaphore_signal(barrier, inc=1, device_id={"red": spot - 1}, device_id_type=MESH)
-
-    @pl.when(spot < count - 1)
-    def _():
-        pl.semaphore_signal(barrier, inc=1, device_id={"red": spot + 1}, device_id_type=MESH)
+    for partner in partners(count):
+        pl.semaphore_signal(barrier, inc=1, device_id={"red": partner}, device_id_type=MESH)
 
 
 def meet(devices, count):
-    spot = lax.axis_index("red")
-    neighbours = jnp.where(spot > 0, 1, 0) + jnp.where(spot < count - 1, 1, 0)
-    pl.semaphore_wait(pltpu.get_barrier_semaphore(), devices - 1 + neighbours)
-
-
-def exchange(devices, source, target, send_sem, recv_sem, base):
+    pl.semaphore_wait(pltpu.get_barrier_semaphore(), devices - 1 + len(partners(count)))
+
+
+def remote(source, target, send_sem, recv_sem, **where):
+    return pltpu.make_async_remote_copy(
+        src_ref=source,
+        dst_ref=target,
+        send_sem=send_sem,
+        recv_sem=recv_sem,
+        device_id=where,
+        device_id_type=MESH,
+    )
+
+
+def exchange(devices, source, target, send_sem, recv_sem):
     me = lax.axis_index("seq")
-    copies = []
     for step in range(1, devices):
         peer = lax.rem(me + step, devices)
-        copy = pltpu.make_async_remote_copy(
-            src_ref=source(peer),
-            dst_ref=target(me),
-            send_sem=send_sem.at[base + step - 1],
-            recv_sem=recv_sem.at[base + step - 1],
-            device_id={"seq": peer},
-            device_id_type=MESH,
-        )
-        copy.start()
-        copies.append(copy)
-    return copies
+        remote(source(peer), target(me), send_sem, recv_sem, seq=peer).start()
+
+
+def semaphores(chunks, count):
+    counts = {
+        "load": 7 + count, "signals": 2, "answers": 2, "reduce": 1, "gather": 1,
+        "same0": chunks * PIECES, "same1": chunks, "same2": chunks * PIECES,
+        "cross0": chunks * PIECES, "cross1": chunks,
+        "near": chunks * PIECES, "far": chunks * PIECES, "relay": chunks,
+    }
+    bases, total = {}, 0
+    for name, needed in counts.items():
+        bases[name] = total
+        total += needed
+    return bases, total
 
 
 def chunk_sizes(piece):
@@ -189,10 +201,8 @@
     tok_hbm, emb_hbm, wt_hbm, filt_hbm, cot_hbm, high_hbm, low_hbm, turn_hbm,
     out_ref, fgrad_ref, grads_ref, weight_ref,
     tok_ref, emb_ref, wt_ref, filt_ref, cot_ref, high_ref, low_ref, turn_ref,
-    part, from_left, from_right, all_ref, out_sig, sig, sending, recv, one_hot,
-    load_sem, wt_sem, sig_send, sig_recv, res_send, res_recv,
-    right_send, right_recv, left_send, left_recv,
-    up_send, up_recv, down_send, down_recv,
+    part, from_same, from_cross, all_ref, out_sig, sig, sending, recv, one_hot,
+    sems,
 ):
     me = lax.axis_index("seq")
     spot = lax.axis_index("red")
@@ -203,13 +213,36 @@
     starts = [sum(sizes[:at]) for at in range(len(sizes))]
     chunks = len(sizes)
     last = count - 1
+    same, cross = partners(count)
+    bases, _ = semaphores(chunks, count)
+
+    def sem(name, index=0):
+        return sems.at[bases[name] + index]
+
+    low_half = spot * 2 < count
+    end = jnp.where(low_half, 0, last)
+    middle = jnp.where(low_half, 1, last - 1)
+    far_middle = last - middle
+    far_end = last - end
+    outer = spot == end
+    inner = spot == middle
     greet(devices, count)
 
+    def pick(at_end, at_middle):
+        return jnp.where(outer, at_end, at_middle)
+
+    orders = [
+        pick(far_middle if REDUCE_DIRECT[0] else far_end, far_end),
+        pick(far_end if REDUCE_DIRECT[0] else far_middle, far_middle),
+        pick(middle, end),
+        spot,
+    ]
+
     def goal_at(index):
-        return jnp.where(spot * 2 < count, last - index, index)
+        return orders[index]
 
     def load(index, source, target):
-        copy = pltpu.make_async_copy(source, target, load_sem.at[index])
+        copy = pltpu.make_async_copy(source, target, sem("load", index))
         copy.start()
         return copy
 
@@ -217,46 +250,49 @@
     wt_loads = []
     for index in range(count):
         goal = goal_at(index)
-        copy = pltpu.make_async_copy(wt_hbm.at[:, goal], wt_ref.at[:, goal], wt_sem.at[index])
-        copy.start()
-        wt_loads.append(copy)
+        wt_loads.append(load(7 + index, wt_hbm.at[:, goal], wt_ref.at[:, goal]))
     signal_loads = [
         load(1, filt_hbm, filt_ref), load(2, cot_hbm, cot_ref), load(3, tok_hbm, tok_ref),
     ]
     table_loads = [
         load(4, high_hbm, high_ref), load(5, low_hbm, low_ref), load(6, turn_hbm, turn_ref),
     ]
-    above_spot = jnp.minimum(spot + 1, last)
-    below_spot = jnp.maximum(spot - 1, 0)
-
-    def view(ref, chunk, group):
-        return ref.at[group, pl.ds(branches * starts[chunk], branches * sizes[chunk])]
-
-    def hop(source, target, chunk, group, sends, recvs, neighbour):
-        slot = chunk * count + group
-        return pltpu.make_async_remote_copy(
-            src_ref=view(source, chunk, group),
-            dst_ref=view(target, chunk, group),
-            send_sem=sends.at[slot],
-            recv_sem=recvs.at[slot],
-            device_id={"red": neighbour},
-            device_id_type=MESH,
+    def view(ref, chunk, group, at=None):
+        rows = branches * sizes[chunk]
+        base = branches * starts[chunk]
+        if at is not None:
+            rows //= PIECES
+            base += at * rows
+        return ref.at[group, pl.ds(base, rows)]
+
+    def slot(name, chunk, at):
+        if name in ("same1", "cross1", "relay"):
+            return sem(name, chunk)
+        return sem(name, chunk * PIECES + at)
+
+    def to_same(kind, chunk, group, at=None):
+        return remote(
+            view(part, chunk, group, at), view(from_same, chunk, group, at),
+            sem("reduce"), slot(f"same{kind}", chunk, at), red=same,
         )
 
-    def right(chunk, group):
-        return hop(part, from_left, chunk, group, right_send, right_recv, above_spot)
-
-    def left(chunk, group):
-        return hop(part, from_right, chunk, group, left_send, left_recv, below_spot)
-
-    def up(chunk, group):
-        return hop(all_ref, all_ref, chunk, group, up_send, up_recv, above_spot)
-
-    def down(chunk, group):
-        return hop(all_ref, all_ref, chunk, group, down_send, down_recv, below_spot)
-
-    def add(target, source, chunk, group):
-        view(target, chunk, group)[...] = view(target, chunk, group)[...] + view(source, chunk, group)[...]
+    def to_cross(kind, chunk, group, at=None):
+        return remote(
+            view(part, chunk, group, at), view(from_cross, chunk, group, at),
+            sem("reduce"), slot(f"cross{kind}", chunk, at), red=cross,
+        )
+
+    def share_to(name, chunk, group, at, partner):
+        block = view(all_ref, chunk, group, at)
+        return remote(block, block, sem("gather"), slot(name, chunk, at), red=partner)
+
+    def every(make, kind, chunk, group):
+        for at in range(PIECES):
+            make(kind, chunk, group, at).start()
+
+    def add(source, chunk, group, at):
+        piece_ref = view(part, chunk, group, at)
+        piece_ref[...] = piece_ref[...] + view(source, chunk, group, at)[...]
 
     def products(index):
         goal = goal_at(index)
@@ -268,99 +304,105 @@
                 base = branches * start + b * size
                 part[goal, base : base + size] = product[b * piece + start : b * piece + start + size]
 
-    def first_hop(chunk, index):
-        @pl.when(spot == 0)
+    def first_sends(chunk, index):
+        direct = REDUCE_DIRECT[chunk]
+        if index == 0:
+            @pl.when(outer)
+            def _():
+                if direct:
+                    every(to_same, 0, chunk, far_middle)
+                else:
+                    every(to_same, 2, chunk, far_end)
+
+            if direct:
+                @pl.when(inner)
+                def _():
+                    every(to_cross, 0, chunk, far_end)
+
+        if index == 1:
+            @pl.when(outer)
+            def _():
+                if direct:
+                    every(to_cross, 0, chunk, far_end)
+                else:
+                    every(to_same, 0, chunk, far_middle)
+
+        if index == 2:
+            @pl.when(outer)
+            def _():
+                every(to_same, 1, chunk, middle)
+
+    def pass_far(chunk, at):
+        to_same(2, chunk, far_end, at).wait_recv()
+        add(from_same, chunk, far_end, at)
+        to_cross(0, chunk, far_end, at).start()
+
+    def pass_cross(chunk, at):
+        to_same(0, chunk, far_middle, at).wait_recv()
+        add(from_same, chunk, far_middle, at)
+        to_cross(1, chunk, far_middle, at).start()
+
+    def pass_same(chunk, at):
+        to_cross(0, chunk, end, at).wait_recv()
+        add(from_cross, chunk, end, at)
+        to_same(0, chunk, end, at).start()
+
+    def arrive(chunk):
+        @pl.when(inner)
         def _():
-            right(chunk, last - index).start()
-
-        @pl.when(spot == last)
+            to_same(1, chunk, spot).wait_recv()
+            to_cross(1, chunk, spot).wait_recv()
+
+        @pl.when(outer)
         def _():
-            left(chunk, index).start()
-
-    def middle_hops(chunk):
-        for tick in range(1, last):
-            goal = last - (tick - spot)
-
-            @pl.when((spot > 0) & (tick >= spot) & (spot < goal))
-            def _():
-                right(chunk, goal).wait_recv()
-                add(part, from_left, chunk, goal)
-                right(chunk, goal).start()
-
-            other = tick - (last - spot)
-
-            @pl.when((spot < last) & (other >= 0) & (spot > other))
-            def _():
-                left(chunk, other).wait_recv()
-                add(part, from_right, chunk, other)
-                left(chunk, other).start()
-
-    def arrive(chunk):
-        @pl.when(spot > 0)
+            for at in range(PIECES):
+                to_same(0, chunk, spot, at).wait_recv()
+                if REDUCE_DIRECT[chunk]:
+                    to_cross(0, chunk, spot, at).wait_recv()
+
+        own = view(part, chunk, spot)[...] + view(from_same, chunk, spot)[...]
+        crossed = view(from_cross, chunk, spot)
+        if REDUCE_DIRECT[chunk]:
+            return own + crossed[...]
+
+        @pl.when(outer)
         def _():
-            right(chunk, spot).wait_recv()
-            add(part, from_left, chunk, spot)
-
-        @pl.when(spot < last)
+            crossed[...] = jnp.zeros(crossed.shape, jnp.float32)
+
+        return own + crossed[...]
+
+    def share(chunk):
+        for at in range(PIECES):
+            share_to("near", chunk, spot, at, same).start()
+        for at in range(PIECES):
+            share_to("far", chunk, spot, at, cross).start()
+
+    def relay_same(chunk, at):
+        share_to("far", chunk, far_middle, at, cross).wait_recv()
+        share_to("relay", chunk, far_middle, at, same).start()
+
+    def relay_cross(chunk, at):
+        share_to("near", chunk, end, at, same).wait_recv()
+        share_to("relay", chunk, end, at, cross).start()
+
+    def collect(name, group, role):
+        @pl.when(role)
         def _():
-            left(chunk, spot).wait_recv()
-            add(part, from_right, chunk, spot)
-
-        return view(part, chunk, spot)[...]
-
-    def share(chunk):
-        @pl.when(spot < last)
-        def _():
-            up(chunk, spot).start()
-
-        @pl.when(spot > 0)
-        def _():
-            down(chunk, spot).start()
-
-    def relay(chunk, sources, distance):
-        for source in sources:
-            if source < last:
-                @pl.when((spot < last) & (spot - source == distance))
-                def _():
-                    up(chunk, source).wait_recv()
-                    up(chunk, source).start()
-
-            if source > 0:
-                @pl.when((spot > 0) & (source - spot == distance))
-                def _():
-                    down(chunk, source).wait_recv()
-                    down(chunk, source).start()
-
-    inner = list(range(1, last))
-    ends = [0, last]
-
-    def relay_far(chunk):
-        for distance in range(2, last):
-            relay(chunk, range(count), distance)
-
-    def collect(chunk):
-        for step in range(1, count):
-            @pl.when(spot == 0)
-            def _():
-                down(chunk, step).wait_recv()
-
-            @pl.when(spot == last)
-            def _():
-                up(chunk, last - step).wait_recv()
-
-    def weights(chunk):
-        start, size = starts[chunk], sizes[chunk]
-        blocks = jnp.concatenate([view(all_ref, chunk, group)[...] for group in range(count)], axis=0)
-        product = dot_split(blocks, emb_ref[...]) * scale_factor
-        for group in range(count):
+            for chunk in range(chunks):
+                for at in [None] if name == "relay" else range(PIECES):
+                    share_to(name, chunk, group, at, same).wait_recv()
+
+    def weights(group):
+        product = dot_split(all_ref[group], emb_ref[...]) * scale_factor
+        for start, size in zip(starts, sizes):
             for b in range(branches):
-                base = (group * branches + b) * size
+                base = branches * start + b * size
                 weight_ref[b, group, start : start + size] = product[base : base + size]
 
     def signal_rows(start, rows, at):
         return sig[at, start : start + rows]
 
-    def channels(chunk, own):
+    def channels(chunk, own, hook):
         start, size = starts[chunk], sizes[chunk]
         projected = dot_split(own, one_hot[...])
         pieces = []
@@ -376,6 +418,7 @@
                 )
             )
         results = convolve(pieces, high_ref, low_ref, turn_ref, size)
+        hook()
         rounded = []
         for at in range(devices):
             queries, key_rows, value_rows, cotangent = held[at]
@@ -403,7 +446,7 @@
     emb_load.wait()
     products(0)
     meet(devices, count)
-    first_hop(0, 0)
+    first_sends(0, 0)
     for copy in signal_loads:
         copy.wait()
     filt_t = filt_ref[...].T
@@ -413,82 +456,115 @@
         out_sig[peer, :piece] = filt_t[peer * piece : (peer + 1) * piece]
         out_sig[peer, piece : 2 * piece] = cot_t[peer * piece : (peer + 1) * piece]
         out_sig[peer, 2 * piece :] = tok_rows
-    copies = exchange(devices, out_sig.at.__getitem__, sig.at.__getitem__, sig_send, sig_recv, 0)
+    exchange(devices, out_sig.at.__getitem__, sig.at.__getitem__, sem("signals"), sem("signals", 1))
     for index in range(1, count):
         products(index)
-        if index < last:
-            first_hop(0, index)
-    for chunk in range(1, chunks):
-        for index in range(last):
-            first_hop(chunk, index)
+        first_sends(0, index)
+    for index in range(count):
+        first_sends(1, index)
     sig[me] = out_sig[me]
-    sent = list(copies)
-    arrivals = []
-    for chunk in range(chunks):
-        middle_hops(chunk)
-        if chunk > 0:
-            relay(chunk - 1, inner, 1)
+    others = pl.ds(0, devices - 1)
+    signals = remote(out_sig.at[others], sig.at[others], sem("signals"), sem("signals", 1), red=same)
+    answers = remote(sending.at[others], recv.at[others], sem("answers"), sem("answers", 1), red=same)
+
+    @pl.when(inner)
+    def _():
+        if REDUCE_DIRECT[0]:
+            for at in range(PIECES):
+                pass_cross(0, at)
+                pass_same(0, at)
         else:
-            for copy in copies:
-                copy.wait_recv()
-            ids = jnp.concatenate([signal_rows(2 * piece, 1, at) for at in range(devices)], axis=1)
-            vocab_rows = lax.broadcasted_iota(jnp.int32, (vocabulary, devices * tok_count), 0)
-            one_hot[...] = jnp.where(vocab_rows == ids.astype(jnp.int32), 1.0, 0.0).astype(jnp.bfloat16)
-            for copy in table_loads:
-                copy.wait()
-        channels(chunk, arrive(chunk))
+            for at in range(PIECES):
+                pass_far(0, at)
+            for at in range(PIECES):
+                pass_same(0, at)
+                pass_cross(0, at)
+        if REDUCE_DIRECT[1]:
+            for at in range(PIECES):
+                pass_same(1, at)
+
+    signals.wait_recv()
+    ids = jnp.concatenate([signal_rows(2 * piece, 1, at) for at in range(devices)], axis=1)
+    vocab_rows = lax.broadcasted_iota(jnp.int32, (vocabulary, devices * tok_count), 0)
+    one_hot[...] = jnp.where(vocab_rows == ids.astype(jnp.int32), 1.0, 0.0).astype(jnp.bfloat16)
+    for copy in table_loads:
+        copy.wait()
+
+    def reduce_hook():
+        @pl.when(inner)
+        def _():
+            if REDUCE_DIRECT[1]:
+                for at in range(PIECES):
+                    pass_cross(1, at)
+            else:
+                for at in range(PIECES):
+                    pass_far(1, at)
+
+    def gather_hook():
+        @pl.when(inner)
+        def _():
+            for at in range(PIECES):
+                relay_same(0, at)
+
+    for chunk, hook in enumerate([reduce_hook, gather_hook]):
+        if chunk == 1 and not REDUCE_DIRECT[1]:
+            @pl.when(inner)
+            def _():
+                for at in range(PIECES):
+                    pass_same(1, at)
+                    pass_cross(1, at)
+
+        channels(chunk, arrive(chunk), hook)
         share(chunk)
         rows = pl.ds(5 * starts[chunk], 5 * sizes[chunk])
-        more = exchange(
+        exchange(
             devices,
             lambda peer, rows=rows: sending.at[peer, rows],
             lambda slot, rows=rows: recv.at[slot, rows],
-            res_send, res_recv, chunk * (devices - 1),
+            sem("answers"), sem("answers", 1),
         )
         recv[me, 5 * starts[chunk] : 5 * (starts[chunk] + sizes[chunk])] = sending[
             me, 5 * starts[chunk] : 5 * (starts[chunk] + sizes[chunk])
         ]
-        sent += more
-        arrivals += more
-    final = chunks - 1
-    for chunk in range(final):
-        relay(chunk, ends, 1)
-    relay(final, inner, 1)
-    for chunk in range(final):
-        relay_far(chunk)
-    for chunk in range(final):
-        collect(chunk)
-        weights(chunk)
-    relay(final, ends, 1)
-    for copy in arrivals:
-        copy.wait_recv()
+
+    @pl.when(inner)
+    def _():
+        for at in range(PIECES):
+            relay_cross(0, at)
+
+    weights(spot)
+
+    @pl.when(inner)
+    def _():
+        for at in range(PIECES):
+            relay_cross(1, at)
+            relay_same(1, at)
+
+    answers.wait_recv()
     out_ref[...] = positions(0)
     fgrad_ref[...] = positions(1)
     for branch in range(branches):
         grads_ref[branch] = positions(2 + branch).astype(jnp.bfloat16)
-    relay_far(final)
-    collect(final)
-    weights(final)
-    for chunk in range(chunks):
-        for group in range(count):
-            @pl.when(spot < group)
-            def _():
-                right(chunk, group).wait_send()
-
-            @pl.when(spot > group)
-            def _():
-                left(chunk, group).wait_send()
-
-            @pl.when((spot >= group) & (spot < last))
-            def _():
-                up(chunk, group).wait_send()
-
-            @pl.when((spot <= group) & (spot > 0))
-            def _():
-                down(chunk, group).wait_send()
-
-    for copy in sent:
-        copy.wait_send()
+    collect("near", middle, outer)
+    weights(pick(middle, end))
+    collect("far", far_end, outer)
+    weights(pick(far_end, far_middle))
+    collect("relay", pick(far_middle, far_end), outer | inner)
+    weights(pick(far_middle, far_end))
+    reduced = pl.ds(0, last)
+    remote(part.at[reduced], from_same.at[reduced], sem("reduce"), sem("same0"), red=same).wait_send()
+
+    @pl.when(outer)
+    def _():
+        pair = all_ref.at[pl.ds(0, 2)]
+        remote(pair, pair, sem("gather"), sem("near"), red=same).wait_send()
+
+    @pl.when(inner)
+    def _():
+        remote(all_ref, all_ref, sem("gather"), sem("near"), red=same).wait_send()
+
+    signals.wait_send()
+    answers.wait_send()
 
 
 def final_kernel(out_in, fgrad_in, grads_in, weight_in, out_ref, fgrad_ref, grads_ref, weight_ref, sem):
@@ -547,14 +623,8 @@
             pltpu.VMEM(answer, f32),
             pltpu.VMEM(answer, f32),
             pltpu.VMEM((vocabulary, devices * tok_count), bf16),
-            dma((7,)),
-            dma((count,)),
-            dma((devices - 1,)),
-            dma((devices - 1,)),
-            dma((chunks * (devices - 1),)),
-            dma((chunks * (devices - 1),)),
-        ]
-        + [dma((chunks * count,))] * 8,
+            dma((semaphores(chunks, count)[1],)),
+        ],
         compiler_params=pltpu.CompilerParams(
             collective_id=0, has_side_effects=True, vmem_limit_bytes=VMEM_BYTES - kept
         ),
@@ -585,13 +655,13 @@
     vocabulary, depth = embedding.shape
     _, branches, red_count, piece = proj_weight.shape
     lanes = (tok_count, vocabulary, depth)
-    aligned = all(size % 128 == 0 for size in lanes) and piece % (8 * sum(SHARES)) == 0
+    aligned = all(size % 128 == 0 for size in lanes) and piece % (8 * sum(SHARES)) == 0 and branches * piece % (8 * sum(SHARES) * PIECES) == 0
     one_hot = vocabulary * tok_count * devices * 8
     held = 4 * branches * piece * (4 * count * vocabulary + 2 * count * depth)
     sides = 4 * tok_count * devices * 20 * piece + 16 * vocabulary * depth
     return (
         aligned
-        and count > 1
+        and count == 4
         and branches == 3
         and red_count == count
         and width == devices * piece

time: 41.6 us -> 36.3 us (0.87)
  Pallas kernels: 40.8 us -> 35.5 us
    pallas_call x1, Pallas kernels: 39.4 us -> 34.2 us  [kernel_shards(): pl.pallas_call(functools.partial(main_kernel, devices, count, scale_facto...]
where the time goes in v3:
time: 36.3 us; the launch traced here: 36.1 us
  Pallas kernels  35.5 us (98%)
  between operations  0.64 us (2%)
    pallas_call x1, Pallas kernels, kernel_shards(): pl.pallas_call(functools.partial(main_kernel, devices, count, scale_facto...  34.2 us
    pallas_call x1, Pallas kernels, kernel_shards(): pl.pallas_call(final_kernel, out_shape=tuple((jax.ShapeDtypeStruct(shape,...  1.32 us

profile of v3, /device:TPU:0, one launch (start us, length us, event | category | flops | bytes accessed | tf_op | source)
XLA Modules:
  0.0 36.1 jit_solution(13637954766514148381)
XLA Ops:
  0.6 34.2 %hyena_exchange.1 = (f32[128,256]{1,0:T(8,128)S(1)}, f32[128,256]{1,0:T(8,128)S(1)}, bf16[3,128,256]{2,1,0:T(8,128)(2,1)S(1)}, f32[3,4,32,1024]{3,2,1,0:T(8,128)S(1)}) custom-call(s32[1,128]{1,0:T(1,128)} %bitcast.5, bf16[512,1024]{1,0:T(8,128)(2,1)} %emb_hbm.1, bf16[3,4,32,1024]{3,2,1,0:T(8,128)(2,1)} %bitcast.4, f32[128,256]{1,0:T(8,128)} %filt_hbm.1, ...), custom_call_target="tpu_custom_call" | custom-call | tf_op jit(solution)/shard_map/hyena_exchange/pallas_call | solution.py:603
  34.8 1.3 %finish.1 = (f32[128,256]{1,0:T(8,128)}, f32[128,256]{1,0:T(8,128)}, bf16[3,128,256]{2,1,0:T(8,128)(2,1)}, f32[3,4,32,1024]{3,2,1,0:T(8,128)}) custom-call(f32[128,256]{1,0:T(8,128)S(1)} %get-tuple-element.12.out_in, f32[128,256]{1,0:T(8,128)S(1)} %get-tuple-element.13.fgrad_in, bf16[3,128,256]{2,1,0:T(8,128)(2,1)S(1)} %get-tuple-element.14.grads_in, ...), custom_call_target="tpu_custom_call" | custom-call | tf_op jit(solution)/shard_map/finish/pallas_call | solution.py:636

commit v4 on v3

--- a/solution.py
+++ b/solution.py
@@ -14,6 +14,11 @@
 VMEM = pl.BlockSpec(memory_space=pltpu.VMEM)
 SHARES = (1, 1)
 REDUCE_DIRECT = (False, True)
+EARLY = True
+ORDERB = True
+STAGE = True
+HOOK = 'after'
+FARFIRST = (0, 1)
 PIECES = 3
 VMEM_BYTES = 67043328
 NN = (((1,), (0,)), ((), ()))
@@ -372,10 +377,20 @@
         return own + crossed[...]
 
     def share(chunk):
-        for at in range(PIECES):
-            share_to("near", chunk, spot, at, same).start()
-        for at in range(PIECES):
-            share_to("far", chunk, spot, at, cross).start()
+        def near():
+            for at in range(PIECES):
+                share_to("near", chunk, spot, at, same).start()
+
+        def far():
+            for at in range(PIECES):
+                share_to("far", chunk, spot, at, cross).start()
+
+        if chunk in FARFIRST:
+            far()
+            near()
+        else:
+            near()
+            far()
 
     def relay_same(chunk, at):
         share_to("far", chunk, far_middle, at, cross).wait_recv()
@@ -460,7 +475,7 @@
     for index in range(1, count):
         products(index)
         first_sends(0, index)
-    for index in range(count):
+    for index in ((0, 2, 1) if ORDERB else (0, 1, 2)):
         first_sends(1, index)
     sig[me] = out_sig[me]
     others = pl.ds(0, devices - 1)
@@ -476,9 +491,15 @@
         else:
             for at in range(PIECES):
                 pass_far(0, at)
-            for at in range(PIECES):
-                pass_same(0, at)
-                pass_cross(0, at)
+            if STAGE:
+                for at in range(PIECES):
+                    pass_cross(0, at)
+                for at in range(PIECES):
+                    pass_same(0, at)
+            else:
+                for at in range(PIECES):
+                    pass_same(0, at)
+                    pass_cross(0, at)
         if REDUCE_DIRECT[1]:
             for at in range(PIECES):
                 pass_same(1, at)
@@ -490,7 +511,16 @@
     for copy in table_loads:
         copy.wait()
 
+    if EARLY:
+        @pl.when(inner)
+        def _():
+            for at in range(PIECES):
+                pass_cross(1, at)
+
     def reduce_hook():
+        if EARLY:
+            return
+
         @pl.when(inner)
         def _():
             if REDUCE_DIRECT[1]:
@@ -501,6 +531,9 @@
                     pass_far(1, at)
 
     def gather_hook():
+        if HOOK == 'after':
+            return
+
         @pl.when(inner)
         def _():
             for at in range(PIECES):
@@ -531,6 +564,9 @@
     def _():
         for at in range(PIECES):
             relay_cross(0, at)
+        if HOOK == 'after':
+            for at in range(PIECES):
+                relay_same(0, at)
 
     weights(spot)
 

time: 36.3 us -> 35.9 us (0.989)
  Pallas kernels: 35.5 us -> 35.1 us
    pallas_call x1, Pallas kernels: 34.2 us -> 33.7 us  [kernel_shards(): pl.pallas_call(functools.partial(main_kernel, devices, count, scale_facto...]
where the time goes in v4:
time: 35.9 us; the launch traced here: 35.7 us
  Pallas kernels  35.1 us (98%)
  between operations  0.64 us (2%)
    pallas_call x1, Pallas kernels, kernel_shards(): pl.pallas_call(functools.partial(main_kernel, devices, count, scale_facto...  33.7 us
    pallas_call x1, Pallas kernels, kernel_shards(): pl.pallas_call(final_kernel, out_shape=tuple((jax.ShapeDtypeStruct(shape,...  1.32 us

profile of v4, /device:TPU:0, one launch (start us, length us, event | category | flops | bytes accessed | tf_op | source)
XLA Modules:
  0.0 35.7 jit_solution(233607848875336985)
XLA Ops:
  0.6 33.7 %hyena_exchange.1 = (f32[128,256]{1,0:T(8,128)S(1)}, f32[128,256]{1,0:T(8,128)S(1)}, bf16[3,128,256]{2,1,0:T(8,128)(2,1)S(1)}, f32[3,4,32,1024]{3,2,1,0:T(8,128)S(1)}) custom-call(s32[1,128]{1,0:T(1,128)} %bitcast.5, bf16[512,1024]{1,0:T(8,128)(2,1)} %emb_hbm.1, bf16[3,4,32,1024]{3,2,1,0:T(8,128)(2,1)} %bitcast.4, f32[128,256]{1,0:T(8,128)} %filt_hbm.1, ...), custom_call_target="tpu_custom_call" | custom-call | tf_op jit(solution)/shard_map/hyena_exchange/pallas_call | solution.py:639
  34.4 1.3 %finish.1 = (f32[128,256]{1,0:T(8,128)}, f32[128,256]{1,0:T(8,128)}, bf16[3,128,256]{2,1,0:T(8,128)(2,1)}, f32[3,4,32,1024]{3,2,1,0:T(8,128)}) custom-call(f32[128,256]{1,0:T(8,128)S(1)} %get-tuple-element.12.out_in, f32[128,256]{1,0:T(8,128)S(1)} %get-tuple-element.13.fgrad_in, bf16[3,128,256]{2,1,0:T(8,128)(2,1)S(1)} %get-tuple-element.14.grads_in, ...), custom_call_target="tpu_custom_call" | custom-call | tf_op jit(solution)/shard_map/finish/pallas_call | solution.py:672

commit v5 on v4

--- a/solution.py
+++ b/solution.py
@@ -18,7 +18,7 @@
 ORDERB = True
 STAGE = True
 HOOK = 'after'
-FARFIRST = (0, 1)
+FARFIRST = ()
 PIECES = 3
 VMEM_BYTES = 67043328
 NN = (((1,), (0,)), ((), ()))
@@ -86,16 +86,48 @@
     return total
 
 
-def fold(pieces, residue, blocks):
+def fold(pieces, residue, blocks, pairs):
     cosines, sines = phases(residue, blocks)
-    return weighted(pieces, cosines), weighted(pieces, sines)
-
-
-def combine(spectrum, block, sub, first):
-    cos_part = spectrum[:, :block]
-    sin_part = spectrum[:, block:]
-    fc, ic, uc = (cos_part[at * sub : (at + 1) * sub] for at in range(3))
-    fs, i_s, us = (sin_part[at * sub : (at + 1) * sub] for at in range(3))
+    half = blocks // 2
+    if residue == 0 or blocks % 2:
+        return weighted(pieces, cosines), weighted(pieces, sines)
+    sums, gaps = pairs
+    real, imag = (sums, gaps) if residue % 2 == 0 else (gaps, sums)
+    at = range(1, half)
+    return (
+        weighted([pieces[0], pieces[half]] + [real[i] for i in at], [1.0, cosines[half]] + [cosines[i] for i in at]),
+        weighted([pieces[half]] + [imag[i] for i in at], [sines[half]] + [sines[i] for i in at]),
+    )
+
+
+def turns_of(turn_ref):
+    blocks = turn_ref.shape[0] // 2
+    return [(turn_ref[at : at + 1], turn_ref[blocks + at : blocks + at + 1]) for at in range(blocks)]
+
+
+def forward(pieces, high_ref, low_ref, turn_ref):
+    blocks = len(pieces)
+    turns = turns_of(turn_ref)
+    inside = range(1, blocks // 2)
+    pairs = (
+        {i: pieces[i] + pieces[blocks - i] for i in inside},
+        {i: pieces[i] - pieces[blocks - i] for i in inside},
+    )
+    first = dot_both(jnp.concatenate(fold(pieces, 0, blocks, pairs), axis=1), high_ref[0], low_ref[0])
+    packed = []
+    for residue in range(1, blocks):
+        even, odd = fold(pieces, residue, blocks, pairs)
+        cosine, sine = turns[residue]
+        packed.append(
+            jnp.concatenate([even * cosine - odd * sine, even * sine + odd * cosine], axis=1)
+        )
+    return first, dot_both(jnp.concatenate(packed, axis=0), high_ref[1], low_ref[1])
+
+
+def combine(kernel, spectrum, block, sub, first):
+    fc, fs = kernel[:, :block], kernel[:, block:]
+    ic, uc = (spectrum[at * sub : (at + 1) * sub, :block] for at in range(2))
+    i_s, us = (spectrum[at * sub : (at + 1) * sub, block:] for at in range(2))
     cc = [fc * ic, fc * uc, uc * ic]
     ss = [fs * i_s, fs * us, us * i_s]
     new_cos = [cc[0] - ss[0], cc[1] + ss[1], cc[2] + ss[2]]
@@ -109,40 +141,46 @@
     return jnp.concatenate([new_cos, new_sin], axis=1)
 
 
-def convolve(pieces, high_ref, low_ref, turn_ref, sub):
+def convolve(pieces, kernel_first, kernel_rest, high_ref, low_ref, turn_ref, sub):
     blocks = len(pieces)
     block = pieces[0].shape[1]
     rows = 3 * sub
     scale = 1.0 / (blocks * block)
-    turns = [(turn_ref[at : at + 1], turn_ref[blocks + at : blocks + at + 1]) for at in range(blocks)]
-    first = dot_both(jnp.concatenate(fold(pieces, 0, blocks), axis=1), high_ref[0], low_ref[0])
-    packed = []
-    for residue in range(1, blocks):
-        even, odd = fold(pieces, residue, blocks)
-        cosine, sine = turns[residue]
-        packed.append(
-            jnp.concatenate([even * cosine - odd * sine, even * sine + odd * cosine], axis=1)
-        )
-    spectrum = dot_both(jnp.concatenate(packed, axis=0), high_ref[1], low_ref[1])
+    turns = turns_of(turn_ref)
+    first, spectrum = forward(pieces, high_ref, low_ref, turn_ref)
     joined = [
-        combine(spectrum[at * rows : (at + 1) * rows], block, sub, False) * scale
+        combine(
+            kernel_rest[at * sub : (at + 1) * sub],
+            spectrum[at * 2 * sub : (at + 1) * 2 * sub],
+            block, sub, False,
+        ) * scale
         for at in range(blocks - 1)
     ]
-    head = dot_both(combine(first, block, sub, True) * scale, high_ref[0], low_ref[0], NT)
+    head = dot_both(combine(kernel_first, first, block, sub, True) * scale, high_ref[0], low_ref[0], NT)
     back = dot_both(jnp.concatenate(joined, axis=0), high_ref[1], low_ref[1], NT)
     cosines, sines = phases(0, blocks)
     results = [
         weighted([head[:, :block], head[:, block:]], [cosines[at], sines[at]])
         for at in range(blocks)
     ]
+    half = blocks // 2
+    pairs = []
     for residue in range(1, blocks):
         real = back[(residue - 1) * rows : residue * rows, :block]
         imag = back[(residue - 1) * rows : residue * rows, block:]
         cosine, sine = turns[residue]
-        cosines, sines = phases(residue, blocks)
-        pair = [real * cosine + imag * sine, imag * cosine - real * sine]
-        for at in range(blocks):
-            results[at] = results[at] + weighted(pair, [cosines[at], sines[at]])
+        pairs.append((real * cosine + imag * sine, imag * cosine - real * sine))
+    for at in range(half + 1):
+        parts = [[], []]
+        for residue in range(1, blocks):
+            cosines, sines = phases(residue, blocks)
+            real, imag = pairs[residue - 1]
+            parts[residue % 2].append((real, cosines[at]))
+            parts[1 - residue % 2].append((imag, sines[at]))
+        equal, turned = (weighted(*zip(*part)) for part in parts)
+        results[at] = results[at] + (equal if turned is None else equal + turned)
+        if 0 < at < half:
+            results[blocks - at] = results[blocks - at] + (equal - turned)
     return results
 
 
@@ -206,7 +244,7 @@
     tok_hbm, emb_hbm, wt_hbm, filt_hbm, cot_hbm, high_hbm, low_hbm, turn_hbm,
     out_ref, fgrad_ref, grads_ref, weight_ref,
     tok_ref, emb_ref, wt_ref, filt_ref, cot_ref, high_ref, low_ref, turn_ref,
-    part, from_same, from_cross, all_ref, out_sig, sig, sending, recv, one_hot,
+    part, from_same, from_cross, all_ref, out_sig, sig, sending, recv, one_hot, spectra,
     sems,
 ):
     me = lax.axis_index("seq")
@@ -417,6 +455,14 @@
     def signal_rows(start, rows, at):
         return sig[at, start : start + rows]
 
+    def transform_filters(chunk):
+        start, size = starts[chunk], sizes[chunk]
+        pieces = [signal_rows(start, size, at) for at in range(devices)]
+        first, rest = forward(pieces, high_ref, low_ref, turn_ref)
+        base = devices * start
+        spectra[base : base + size] = first
+        spectra[base + size : base + devices * size] = rest
+
     def channels(chunk, own, hook):
         start, size = starts[chunk], sizes[chunk]
         projected = dot_split(own, one_hot[...])
@@ -428,11 +474,14 @@
             cotangent = signal_rows(piece + start, size, at)
             held.append((queries, key_rows, value_rows, cotangent))
             pieces.append(
-                jnp.concatenate(
-                    [signal_rows(start, size, at), key_rows * value_rows, cotangent * queries], axis=0
-                )
+                jnp.concatenate([key_rows * value_rows, cotangent * queries], axis=0)
             )
-        results = convolve(pieces, high_ref, low_ref, turn_ref, size)
+        base = devices * start
+        kernel_first = spectra[base : base + size]
+        kernel_rest = spectra[base + size : base + devices * size]
+        results = convolve(
+            pieces, kernel_first, kernel_rest, high_ref, low_ref, turn_ref, size
+        )
         hook()
         rounded = []
         for at in range(devices):
@@ -510,6 +559,8 @@
     one_hot[...] = jnp.where(vocab_rows == ids.astype(jnp.int32), 1.0, 0.0).astype(jnp.bfloat16)
     for copy in table_loads:
         copy.wait()
+    for chunk in range(chunks):
+        transform_filters(chunk)
 
     if EARLY:
         @pl.when(inner)
@@ -659,6 +710,7 @@
             pltpu.VMEM(answer, f32),
             pltpu.VMEM(answer, f32),
             pltpu.VMEM((vocabulary, devices * tok_count), bf16),
+            pltpu.VMEM((devices * piece, 2 * tok_count), f32),
             dma((semaphores(chunks, count)[1],)),
         ],
         compiler_params=pltpu.CompilerParams(
@@ -701,6 +753,7 @@
         and branches == 3
         and red_count == count
         and width == devices * piece
+        and devices % 2 == 0
         and one_hot + held + sides < 36 * 2**20
     )
 

time: 35.9 us -> 35.9 us (level)
  no operation moved by 1% of the time
where the time goes in v5:
time: 35.9 us; the launch traced here: 35.7 us
  Pallas kernels  35.1 us (98%)
  between operations  0.64 us (2%)
    pallas_call x1, Pallas kernels, kernel_shards(): pl.pallas_call(functools.partial(main_kernel, devices, count, scale_facto...  33.8 us
    pallas_call x1, Pallas kernels, kernel_shards(): pl.pallas_call(final_kernel, out_shape=tuple((jax.ShapeDtypeStruct(shape,...  1.32 us

profile of v5, /device:TPU:0, one launch (start us, length us, event | category | flops | bytes accessed | tf_op | source)
XLA Modules:
  0.0 35.7 jit_solution(2871280459023830359)
XLA Ops:
  0.6 33.8 %hyena_exchange.1 = (f32[128,256]{1,0:T(8,128)S(1)}, f32[128,256]{1,0:T(8,128)S(1)}, bf16[3,128,256]{2,1,0:T(8,128)(2,1)S(1)}, f32[3,4,32,1024]{3,2,1,0:T(8,128)S(1)}) custom-call(s32[1,128]{1,0:T(1,128)} %bitcast.5, bf16[512,1024]{1,0:T(8,128)(2,1)} %emb_hbm.1, bf16[3,4,32,1024]{3,2,1,0:T(8,128)(2,1)} %bitcast.4, f32[128,256]{1,0:T(8,128)} %filt_hbm.1, ...), custom_call_target="tpu_custom_call" | custom-call | tf_op jit(solution)/shard_map/hyena_exchange/pallas_call | solution.py:690
  34.4 1.3 %finish.1 = (f32[128,256]{1,0:T(8,128)}, f32[128,256]{1,0:T(8,128)}, bf16[3,128,256]{2,1,0:T(8,128)(2,1)}, f32[3,4,32,1024]{3,2,1,0:T(8,128)}) custom-call(f32[128,256]{1,0:T(8,128)S(1)} %get-tuple-element.12.out_in, f32[128,256]{1,0:T(8,128)S(1)} %get-tuple-element.13.fgrad_in, bf16[3,128,256]{2,1,0:T(8,128)(2,1)S(1)} %get-tuple-element.14.grads_in, ...), custom_call_target="tpu_custom_call" | custom-call | tf_op jit(solution)/shard_map/finish/pallas_call | solution.py:724

commit v6 on v4

--- a/solution.py
+++ b/solution.py
@@ -18,7 +18,7 @@
 ORDERB = True
 STAGE = True
 HOOK = 'after'
-FARFIRST = (0, 1)
+FARFIRST = (1,)
 PIECES = 3
 VMEM_BYTES = 67043328
 NN = (((1,), (0,)), ((), ()))
@@ -186,7 +186,7 @@
 def semaphores(chunks, count):
     counts = {
         "load": 7 + count, "signals": 2, "answers": 2, "reduce": 1, "gather": 1,
-        "same0": chunks * PIECES, "same1": chunks, "same2": chunks * PIECES,
+        "same0": chunks * PIECES, "same1": chunks, "same2": PIECES,
         "cross0": chunks * PIECES, "cross1": chunks,
         "near": chunks * PIECES, "far": chunks * PIECES, "relay": chunks,
     }

time: 35.9 us -> 35.8 us (level)
  no operation moved by 1% of the time
where the time goes in v6:
time: 35.8 us; the launch traced here: 35.7 us
  Pallas kernels  35 us (98%)
  between operations  0.64 us (2%)
    pallas_call x1, Pallas kernels, kernel_shards(): pl.pallas_call(functools.partial(main_kernel, devices, count, scale_facto...  33.7 us
    pallas_call x1, Pallas kernels, kernel_shards(): pl.pallas_call(final_kernel, out_shape=tuple((jax.ShapeDtypeStruct(shape,...  1.32 us

profile of v6, /device:TPU:0, one launch (start us, length us, event | category | flops | bytes accessed | tf_op | source)
XLA Modules:
  0.0 35.7 jit_solution(9509674222756367076)
XLA Ops:
  0.6 33.7 %hyena_exchange.1 = (f32[128,256]{1,0:T(8,128)S(1)}, f32[128,256]{1,0:T(8,128)S(1)}, bf16[3,128,256]{2,1,0:T(8,128)(2,1)S(1)}, f32[3,4,32,1024]{3,2,1,0:T(8,128)S(1)}) custom-call(s32[1,128]{1,0:T(1,128)} %bitcast.5, bf16[512,1024]{1,0:T(8,128)(2,1)} %emb_hbm.1, bf16[3,4,32,1024]{3,2,1,0:T(8,128)(2,1)} %bitcast.4, f32[128,256]{1,0:T(8,128)} %filt_hbm.1, ...), custom_call_target="tpu_custom_call" | custom-call | tf_op jit(solution)/shard_map/hyena_exchange/pallas_call | solution.py:639
  34.4 1.3 %finish.1 = (f32[128,256]{1,0:T(8,128)}, f32[128,256]{1,0:T(8,128)}, bf16[3,128,256]{2,1,0:T(8,128)(2,1)}, f32[3,4,32,1024]{3,2,1,0:T(8,128)}) custom-call(f32[128,256]{1,0:T(8,128)S(1)} %get-tuple-element.12.out_in, f32[128,256]{1,0:T(8,128)S(1)} %get-tuple-element.13.fgrad_in, bf16[3,128,256]{2,1,0:T(8,128)(2,1)S(1)} %get-tuple-element.14.grads_in, ...), custom_call_target="tpu_custom_call" | custom-call | tf_op jit(solution)/shard_map/finish/pallas_call | solution.py:672
